TPU v7x, 32 devices: a whole 2x2x4 slice. The times are simulated.
32 devices in a mesh: snap: 8 (over z, core), vtx: 4 (over y, x).
Axes of the slice: x: 2, y: 2, z: 4, core: 2. Of those that a mesh axis runs over, the one named last changes fastest.
Arguments:
- feats: float32 [8, 4096, 512], P('snap', 'vtx'), may hold values from -6 to 6
- col_ids: int32 [8, 32, 16], P('snap', 'vtx'), may hold values from 0 to 31
- tiles: float32 [8, 32, 16, 128, 128], P('snap', 'vtx'), may hold values from -0.125 to 0.125
- w_first: float32 [512, 256], replicated, may hold values from -0.25 to 0.25
- w_input: float32 [256, 1024], replicated, may hold values from -0.375 to 0.375
- w_recur: float32 [256, 1024], replicated, may hold values from -0.375 to 0.375
- lstm_bias: float32 [1024], replicated, may hold values from -3 to 3
- w_second: float32 [256, 256], replicated, may hold values from -0.375 to 0.375
Outputs:
- output: float32 [8, 4096, 256], P('snap', 'vtx')
Inputs may be any that keep to these rules, and one draw needn't show every extreme that they name: `col_ids`: every entry names a row block of the same snapshot's graph; a few blocks are named far more often than others.
All inputs are finite; a program needn't handle non-finite values.
Results may differ from a plain program's by a relative error of at most 0.0003.
Values sent between devices are 32-bit elements; how exact they have to be, the bound alone decides.
No kernel may reach another device: no remote copies, remote signals or barrier semaphores. Data moves between devices by JAX's collectives and lax.ppermute only.
A program may use at most 128 MiB of HBM per device.

v0:
```python
import jax
import jax.numpy as jnp
from jax import lax
from jax.sharding import PartitionSpec as P


def block_sum(tile_set, column_ids, source):
    tile_edge = tile_set.shape[-1]
    width = source.shape[-1]
    blocks = source.reshape(source.shape[0] // tile_edge, tile_edge, width)

    def row_block(operands):
        tiles_here, ids_here = operands
        picked = blocks[ids_here]
        return jnp.einsum("ktu,kuw->tw", tiles_here, picked, precision=lax.Precision.HIGHEST)

    summed = lax.map(row_block, (tile_set, column_ids))
    return summed.reshape(-1, width)


def row_scale(tiles):
    sums = jnp.sum(tiles * tiles, axis=(2, 4))
    return lax.rsqrt(1.0 + sums).reshape(tiles.shape[0], -1)[..., None]


def recurrence(pre_time, w_recur, lstm_bias):
    hidden_size = w_recur.shape[0]

    def advance(carry, pre_step):
        state_h, state_c = carry
        gates = pre_step + jnp.dot(state_h, w_recur, precision=lax.Precision.HIGHEST) + lstm_bias
        gate_i = gates[:, :hidden_size]
        gate_f = gates[:, hidden_size : 2 * hidden_size]
        gate_g = gates[:, 2 * hidden_size : 3 * hidden_size]
        gate_o = gates[:, 3 * hidden_size :]
        state_c = jax.nn.sigmoid(gate_f) * state_c + jax.nn.sigmoid(gate_i) * jnp.tanh(gate_g)
        state_h = jax.nn.sigmoid(gate_o) * jnp.tanh(state_c)
        return ((state_h, state_c), state_h)

    zeros = jnp.zeros((pre_time.shape[1], hidden_size), jnp.float32)
    _, states = lax.scan(advance, (zeros, zeros), pre_time)
    return states


def on_device(feats, col_ids, tiles, w_first, w_input, w_recur, lstm_bias, w_second):
    scale = row_scale(tiles)
    projected = jnp.einsum("svf,fh->svh", feats, w_first, precision=lax.Precision.HIGHEST)
    whole = lax.all_gather(projected, "vtx", axis=1, tiled=True)
    hidden_one = jax.nn.relu(scale * (projected + jax.vmap(block_sum)(tiles, col_ids, whole)))
    timelines = lax.all_to_all(hidden_one, "snap", split_axis=1, concat_axis=0, tiled=True)
    pre_time = jnp.einsum("svh,hg->svg", timelines, w_input, precision=lax.Precision.HIGHEST)
    states = recurrence(pre_time, w_recur, lstm_bias)
    returned = lax.all_to_all(states, "snap", split_axis=0, concat_axis=1, tiled=True)
    whole_two = lax.all_gather(returned, "vtx", axis=1, tiled=True)
    mixed_two = scale * (returned + jax.vmap(block_sum)(tiles, col_ids, whole_two))
    return jnp.einsum("svh,hg->svg", mixed_two, w_second, precision=lax.Precision.HIGHEST)


def solution(mesh):
    placed = (
        P("snap", "vtx", None),
        P("snap", "vtx", None),
        P("snap", "vtx", None, None, None),
        P(),
        P(),
        P(),
        P(),
        P(),
    )
    return jax.shard_map(
        on_device, mesh=mesh, in_specs=placed, out_specs=P("snap", "vtx", None), check_vma=False
    )
```

profile of v0, /device:TPU:0, one launch (start us, length us, event | category | flops | bytes accessed | tf_op | source)
XLA Modules:
  0.0 360.7 jit_solution(10753765310312804185)
XLA Ops:
  8.1 3.8 %fusion.28 = f32[1024,256]{1,0:T(8,128)} fusion(f32[512,256]{1,0:T(8,128)} %param.17, f32[1,1024,512]{2,1,0:T(8,128)S(1)} %copy-done), kind=kOutput, calls=%fused_computation.47 | convolution fusion | flops 1610612736 | bytes 3670016 | tf_op jit(solution)/shard_map/svf,fh->svh/dot_general | solution.py:47
  12.0 4.0 %multiply_reduce_fusion = f32[8,128]{1,0:T(8,128)S(1)} fusion(f32[1,8,16,128,128]{4,3,2,1,0:T(8,128)} %param.16), kind=kLoop, calls=%fused_computation.46 | loop fusion | flops 4193280 | bytes 8392704 | tf_op jit(solution)/shard_map/reduce_sum | solution.py:22
  16.0 51.4 %all-gather.6.cloned.1.call-done = f32[4096,256]{1,0:T(8,128)} async-done(((f32[1024,256]{1,0:T(8,128)}), f32[4096,256]{1,0:T(8,128)}) %all-gather.6.cloned.1.call-update) | async-done | bytes 4194320 | tf_op jit(solution)/shard_map/all_gather | solution.py:48
  68.5 68.9 %while.35 = (s32[]{:T(128)}, f32[8,1,128,256]{3,2,1,0:T(8,128)}, f32[8,1,16,128,128]{4,3,2,1,0:T(8,128)}, s32[8,1,16]{2,1,0:T(1,128)}, f32[1,32,128,256]{3,2,1,0:T(8,128)}, /*index=5*/s32[]{:T(128)}) while((s32[]{:T(128)}, f32[8,1,128,256]{3,2,1,0:T(8,128)}, f32[8,1,16,128,128]{4,3,2,1,0:T(8,128)}, s32[8,1,16]{2,1,0:T(1,128)}, ...), condition=%wide.region_2.3_spmd, body=%wide.region_1.2_spmd.sunk | while | flops 805306496 | bytes 7472841 | solution.py:17
  69.3 4.2 %gather_fusion = f32[16,128,256]{2,1,0:T(8,128)} fusion(f32[1,32,128,256]{3,2,1,0:T(8,128)} %get-tuple-element.307, s32[16]{0:T(128)S(1)} %or_bitcast_fusion.4), kind=kCustom, calls=%fused_computation.clone.1 | custom fusion | bytes 4194432 | tf_op jit(solution)/shard_map/vmap()/while/body/eval_jaxpr/gather | solution.py:14
  73.5 3.7 %fusion.55 = f32[8,1,128,256]{3,2,1,0:T(8,128)} fusion(f32[8,1,128,256]{3,2,1,0:T(8,128)} %get-tuple-element.298, s32[]{:T(128)} %get-tuple-element.297, f32[16,128,256]{2,1,0:T(8,128)} %gather_fusion, f32[8,1,16,128,128]{4,3,2,1,0:T(8,128)} %get-tuple-element.305), kind=kOutput, calls=%fused_computation.3.clone.1 | convolution fusion | flops 805306368 | bytes 3277824 | tf_op jit(solution)/shard_map/vmap()/while/body/eval_jaxpr/ktu,kuw->tw/dot_general | solution.py:15
  77.9 4.2 %gather_fusion = f32[16,128,256]{2,1,0:T(8,128)} fusion(f32[1,32,128,256]{3,2,1,0:T(8,128)} %get-tuple-element.307, s32[16]{0:T(128)S(1)} %or_bitcast_fusion.4), kind=kCustom, calls=%fused_computation.clone.1 | custom fusion | bytes 4194432 | tf_op jit(solution)/shard_map/vmap()/while/body/eval_jaxpr/gather | solution.py:14
  82.1 3.7 %fusion.55 = f32[8,1,128,256]{3,2,1,0:T(8,128)} fusion(f32[8,1,128,256]{3,2,1,0:T(8,128)} %get-tuple-element.298, s32[]{:T(128)} %get-tuple-element.297, f32[16,128,256]{2,1,0:T(8,128)} %gather_fusion, f32[8,1,16,128,128]{4,3,2,1,0:T(8,128)} %get-tuple-element.305), kind=kOutput, calls=%fused_computation.3.clone.1 | convolution fusion | flops 805306368 | bytes 3277824 | tf_op jit(solution)/shard_map/vmap()/while/body/eval_jaxpr/ktu,kuw->tw/dot_general | solution.py:15
  86.5 4.2 %gather_fusion = f32[16,128,256]{2,1,0:T(8,128)} fusion(f32[1,32,128,256]{3,2,1,0:T(8,128)} %get-tuple-element.307, s32[16]{0:T(128)S(1)} %or_bitcast_fusion.4), kind=kCustom, calls=%fused_computation.clone.1 | custom fusion | bytes 4194432 | tf_op jit(solution)/shard_map/vmap()/while/body/eval_jaxpr/gather | solution.py:14
  90.7 3.7 %fusion.55 = f32[8,1,128,256]{3,2,1,0:T(8,128)} fusion(f32[8,1,128,256]{3,2,1,0:T(8,128)} %get-tuple-element.298, s32[]{:T(128)} %get-tuple-element.297, f32[16,128,256]{2,1,0:T(8,128)} %gather_fusion, f32[8,1,16,128,128]{4,3,2,1,0:T(8,128)} %get-tuple-element.305), kind=kOutput, calls=%fused_computation.3.clone.1 | convolution fusion | flops 805306368 | bytes 3277824 | tf_op jit(solution)/shard_map/vmap()/while/body/eval_jaxpr/ktu,kuw->tw/dot_general | solution.py:15
  95.1 4.2 %gather_fusion = f32[16,128,256]{2,1,0:T(8,128)} fusion(f32[1,32,128,256]{3,2,1,0:T(8,128)} %get-tuple-element.307, s32[16]{0:T(128)S(1)} %or_bitcast_fusion.4), kind=kCustom, calls=%fused_computation.clone.1 | custom fusion | bytes 4194432 | tf_op jit(solution)/shard_map/vmap()/while/body/eval_jaxpr/gather | solution.py:14
  99.3 3.7 %fusion.55 = f32[8,1,128,256]{3,2,1,0:T(8,128)} fusion(f32[8,1,128,256]{3,2,1,0:T(8,128)} %get-tuple-element.298, s32[]{:T(128)} %get-tuple-element.297, f32[16,128,256]{2,1,0:T(8,128)} %gather_fusion, f32[8,1,16,128,128]{4,3,2,1,0:T(8,128)} %get-tuple-element.305), kind=kOutput, calls=%fused_computation.3.clone.1 | convolution fusion | flops 805306368 | bytes 3277824 | tf_op jit(solution)/shard_map/vmap()/while/body/eval_jaxpr/ktu,kuw->tw/dot_general | solution.py:15
  103.7 4.2 %gather_fusion = f32[16,128,256]{2,1,0:T(8,128)} fusion(f32[1,32,128,256]{3,2,1,0:T(8,128)} %get-tuple-element.307, s32[16]{0:T(128)S(1)} %or_bitcast_fusion.4), kind=kCustom, calls=%fused_computation.clone.1 | custom fusion | bytes 4194432 | tf_op jit(solution)/shard_map/vmap()/while/body/eval_jaxpr/gather | solution.py:14
  107.9 3.7 %fusion.55 = f32[8,1,128,256]{3,2,1,0:T(8,128)} fusion(f32[8,1,128,256]{3,2,1,0:T(8,128)} %get-tuple-element.298, s32[]{:T(128)} %get-tuple-element.297, f32[16,128,256]{2,1,0:T(8,128)} %gather_fusion, f32[8,1,16,128,128]{4,3,2,1,0:T(8,128)} %get-tuple-element.305), kind=kOutput, calls=%fused_computation.3.clone.1 | convolution fusion | flops 805306368 | bytes 3277824 | tf_op jit(solution)/shard_map/vmap()/while/body/eval_jaxpr/ktu,kuw->tw/dot_general | solution.py:15
  112.3 4.2 %gather_fusion = f32[16,128,256]{2,1,0:T(8,128)} fusion(f32[1,32,128,256]{3,2,1,0:T(8,128)} %get-tuple-element.307, s32[16]{0:T(128)S(1)} %or_bitcast_fusion.4), kind=kCustom, calls=%fused_computation.clone.1 | custom fusion | bytes 4194432 | tf_op jit(solution)/shard_map/vmap()/while/body/eval_jaxpr/gather | solution.py:14
  116.5 3.7 %fusion.55 = f32[8,1,128,256]{3,2,1,0:T(8,128)} fusion(f32[8,1,128,256]{3,2,1,0:T(8,128)} %get-tuple-element.298, s32[]{:T(128)} %get-tuple-element.297, f32[16,128,256]{2,1,0:T(8,128)} %gather_fusion, f32[8,1,16,128,128]{4,3,2,1,0:T(8,128)} %get-tuple-element.305), kind=kOutput, calls=%fused_computation.3.clone.1 | convolution fusion | flops 805306368 | bytes 3277824 | tf_op jit(solution)/shard_map/vmap()/while/body/eval_jaxpr/ktu,kuw->tw/dot_general | solution.py:15
  120.9 4.2 %gather_fusion = f32[16,128,256]{2,1,0:T(8,128)} fusion(f32[1,32,128,256]{3,2,1,0:T(8,128)} %get-tuple-element.307, s32[16]{0:T(128)S(1)} %or_bitcast_fusion.4), kind=kCustom, calls=%fused_computation.clone.1 | custom fusion | bytes 4194432 | tf_op jit(solution)/shard_map/vmap()/while/body/eval_jaxpr/gather | solution.py:14
  125.1 3.7 %fusion.55 = f32[8,1,128,256]{3,2,1,0:T(8,128)} fusion(f32[8,1,128,256]{3,2,1,0:T(8,128)} %get-tuple-element.298, s32[]{:T(128)} %get-tuple-element.297, f32[16,128,256]{2,1,0:T(8,128)} %gather_fusion, f32[8,1,16,128,128]{4,3,2,1,0:T(8,128)} %get-tuple-element.305), kind=kOutput, calls=%fused_computation.3.clone.1 | convolution fusion | flops 805306368 | bytes 3277824 | tf_op jit(solution)/shard_map/vmap()/while/body/eval_jaxpr/ktu,kuw->tw/dot_general | solution.py:15
  129.5 4.2 %gather_fusion = f32[16,128,256]{2,1,0:T(8,128)} fusion(f32[1,32,128,256]{3,2,1,0:T(8,128)} %get-tuple-element.307, s32[16]{0:T(128)S(1)} %or_bitcast_fusion.4), kind=kCustom, calls=%fused_computation.clone.1 | custom fusion | bytes 4194432 | tf_op jit(solution)/shard_map/vmap()/while/body/eval_jaxpr/gather | solution.py:14
  133.7 3.7 %fusion.55 = f32[8,1,128,256]{3,2,1,0:T(8,128)} fusion(f32[8,1,128,256]{3,2,1,0:T(8,128)} %get-tuple-element.298, s32[]{:T(128)} %get-tuple-element.297, f32[16,128,256]{2,1,0:T(8,128)} %gather_fusion, f32[8,1,16,128,128]{4,3,2,1,0:T(8,128)} %get-tuple-element.305), kind=kOutput, calls=%fused_computation.3.clone.1 | convolution fusion | flops 805306368 | bytes 3277824 | tf_op jit(solution)/shard_map/vmap()/while/body/eval_jaxpr/ktu,kuw->tw/dot_general | solution.py:15
  138.8 2.1 copy.12
  140.9 4.6 %all-to-all-start = ((f32[1,1024,256]{2,0,1:T(1,128)}), f32[1,1024,256]{2,0,1:T(1,128)S(1)}, u32[]{:S(2)}, u32[]{:S(2)}) async-start(f32[1,1024,256]{2,0,1:T(1,128)} %copy.12), calls=%async_computation | async-start | bytes 2097152 | tf_op jit(solution)/shard_map/all_to_all | solution.py:50
  145.6 26.5 %all-to-all-done = f32[1,1024,256]{2,0,1:T(1,128)S(1)} async-done(((f32[1,1024,256]{2,0,1:T(1,128)}), f32[1,1024,256]{2,0,1:T(1,128)S(1)}, u32[]{:S(2)}, u32[]{:S(2)}) %all-to-all-start) | async-done | bytes 1048608 | tf_op jit(solution)/shard_map/all_to_all | solution.py:50
  173.3 5.0 %fusion.31 = f32[8,128,1024]{2,1,0:T(8,128)} fusion(f32[8,128,256]{2,1,0:T(8,128)S(1)} %bitcast.112, f32[256,1024]{1,0:T(8,128)S(1)} %copy-done.4), kind=kOutput, calls=%fused_computation.52 | convolution fusion | flops 3221225472 | bytes 6291456 | tf_op jit(solution)/shard_map/svh,hg->svg/dot_general | solution.py:51
  178.3 20.6 %while.37 = (s32[]{:T(128)}, f32[128,256]{1,0:T(8,128)S(1)}, f32[128,256]{1,0:T(8,128)S(1)}, f32[8,128,256]{2,1,0:T(8,128)}, f32[8,128,1024]{2,1,0:T(8,128)}, /*...) while((s32[]{:T(128)}, f32[128,256]{1,0:T(8,128)S(1)}, ...), condition=%wide.region_4.5_spmd.clone, body=%wide.region_3.4_spmd.clone.sunk | while | flops 403406848 | bytes 3281516 | solution.py:41
  183.4 1.8 fusion.61
  188.6 1.8 fusion.61
  193.8 1.8 fusion.61
  198.9 30.8 %all_to_all.27 = f32[8,128,256]{2,1,0:T(8,128)} all-to-all(f32[8,128,256]{2,1,0:T(8,128)} %get-tuple-element.97), channel_id=1, replica_groups=mesh['snap'=8,'vtx'=4] {'snap'}, dimensions={0} | all-to-all | bytes 2097152 | tf_op jit(solution)/shard_map/all_to_all | solution.py:53
  229.7 50.7 %all-gather.4.cloned.1.call-done = f32[1,4096,256]{2,1,0:T(8,128)} async-done(((f32[1,1024,256]{2,1,0:T(8,128)}), f32[1,4096,256]{2,1,0:T(8,128)}) %all-gather.4.cloned.1.call-update) | async-done | bytes 4194320 | tf_op jit(solution)/shard_map/all_gather | solution.py:54
  281.5 68.9 %while.36 = (s32[]{:T(128)}, f32[8,1,128,256]{3,2,1,0:T(8,128)}, f32[8,1,16,128,128]{4,3,2,1,0:T(8,128)}, s32[8,1,16]{2,1,0:T(1,128)}, f32[1,32,128,256]{3,2,1,0:T(8,128)}, /*index=5*/s32[]{:T(128)}) while((s32[]{:T(128)}, f32[8,1,128,256]{3,2,1,0:T(8,128)}, f32[8,1,16,128,128]{4,3,2,1,0:T(8,128)}, s32[8,1,16]{2,1,0:T(1,128)}, ...), condition=%wide.region_6.7_spmd, body=%wide.region_5.6_spmd.sunk | while | flops 805306496 | bytes 7472841 | solution.py:17
  282.2 4.2 %gather_fusion.1 = f32[16,128,256]{2,1,0:T(8,128)} fusion(f32[1,32,128,256]{3,2,1,0:T(8,128)} %get-tuple-element.352, s32[16]{0:T(128)S(1)} %or_bitcast_fusion.5), kind=kCustom, calls=%fused_computation.1.clone.1 | custom fusion | bytes 4194432 | tf_op jit(solution)/shard_map/vmap()/while/body/eval_jaxpr/gather | solution.py:14
  286.5 3.7 %fusion.58 = f32[8,1,128,256]{3,2,1,0:T(8,128)} fusion(f32[8,1,128,256]{3,2,1,0:T(8,128)} %get-tuple-element.343, s32[]{:T(128)} %get-tuple-element.342, f32[16,128,256]{2,1,0:T(8,128)} %gather_fusion.1, f32[8,1,16,128,128]{4,3,2,1,0:T(8,128)} %get-tuple-element.350), kind=kOutput, calls=%fused_computation.13.clone.1 | convolution fusion | flops 805306368 | bytes 3277824 | tf_op jit(solution)/shard_map/vmap()/while/body/eval_jaxpr/ktu,kuw->tw/dot_general | solution.py:15
  290.8 4.2 %gather_fusion.1 = f32[16,128,256]{2,1,0:T(8,128)} fusion(f32[1,32,128,256]{3,2,1,0:T(8,128)} %get-tuple-element.352, s32[16]{0:T(128)S(1)} %or_bitcast_fusion.5), kind=kCustom, calls=%fused_computation.1.clone.1 | custom fusion | bytes 4194432 | tf_op jit(solution)/shard_map/vmap()/while/body/eval_jaxpr/gather | solution.py:14
  295.1 3.7 %fusion.58 = f32[8,1,128,256]{3,2,1,0:T(8,128)} fusion(f32[8,1,128,256]{3,2,1,0:T(8,128)} %get-tuple-element.343, s32[]{:T(128)} %get-tuple-element.342, f32[16,128,256]{2,1,0:T(8,128)} %gather_fusion.1, f32[8,1,16,128,128]{4,3,2,1,0:T(8,128)} %get-tuple-element.350), kind=kOutput, calls=%fused_computation.13.clone.1 | convolution fusion | flops 805306368 | bytes 3277824 | tf_op jit(solution)/shard_map/vmap()/while/body/eval_jaxpr/ktu,kuw->tw/dot_general | solution.py:15
  299.4 4.2 %gather_fusion.1 = f32[16,128,256]{2,1,0:T(8,128)} fusion(f32[1,32,128,256]{3,2,1,0:T(8,128)} %get-tuple-element.352, s32[16]{0:T(128)S(1)} %or_bitcast_fusion.5), kind=kCustom, calls=%fused_computation.1.clone.1 | custom fusion | bytes 4194432 | tf_op jit(solution)/shard_map/vmap()/while/body/eval_jaxpr/gather | solution.py:14
  303.7 3.7 %fusion.58 = f32[8,1,128,256]{3,2,1,0:T(8,128)} fusion(f32[8,1,128,256]{3,2,1,0:T(8,128)} %get-tuple-element.343, s32[]{:T(128)} %get-tuple-element.342, f32[16,128,256]{2,1,0:T(8,128)} %gather_fusion.1, f32[8,1,16,128,128]{4,3,2,1,0:T(8,128)} %get-tuple-element.350), kind=kOutput, calls=%fused_computation.13.clone.1 | convolution fusion | flops 805306368 | bytes 3277824 | tf_op jit(solution)/shard_map/vmap()/while/body/eval_jaxpr/ktu,kuw->tw/dot_general | solution.py:15
  308.0 4.2 %gather_fusion.1 = f32[16,128,256]{2,1,0:T(8,128)} fusion(f32[1,32,128,256]{3,2,1,0:T(8,128)} %get-tuple-element.352, s32[16]{0:T(128)S(1)} %or_bitcast_fusion.5), kind=kCustom, calls=%fused_computation.1.clone.1 | custom fusion | bytes 4194432 | tf_op jit(solution)/shard_map/vmap()/while/body/eval_jaxpr/gather | solution.py:14
  312.3 3.7 %fusion.58 = f32[8,1,128,256]{3,2,1,0:T(8,128)} fusion(f32[8,1,128,256]{3,2,1,0:T(8,128)} %get-tuple-element.343, s32[]{:T(128)} %get-tuple-element.342, f32[16,128,256]{2,1,0:T(8,128)} %gather_fusion.1, f32[8,1,16,128,128]{4,3,2,1,0:T(8,128)} %get-tuple-element.350), kind=kOutput, calls=%fused_computation.13.clone.1 | convolution fusion | flops 805306368 | bytes 3277824 | tf_op jit(solution)/shard_map/vmap()/while/body/eval_jaxpr/ktu,kuw->tw/dot_general | solution.py:15
  316.6 4.2 %gather_fusion.1 = f32[16,128,256]{2,1,0:T(8,128)} fusion(f32[1,32,128,256]{3,2,1,0:T(8,128)} %get-tuple-element.352, s32[16]{0:T(128)S(1)} %or_bitcast_fusion.5), kind=kCustom, calls=%fused_computation.1.clone.1 | custom fusion | bytes 4194432 | tf_op jit(solution)/shard_map/vmap()/while/body/eval_jaxpr/gather | solution.py:14
  320.9 3.7 %fusion.58 = f32[8,1,128,256]{3,2,1,0:T(8,128)} fusion(f32[8,1,128,256]{3,2,1,0:T(8,128)} %get-tuple-element.343, s32[]{:T(128)} %get-tuple-element.342, f32[16,128,256]{2,1,0:T(8,128)} %gather_fusion.1, f32[8,1,16,128,128]{4,3,2,1,0:T(8,128)} %get-tuple-element.350), kind=kOutput, calls=%fused_computation.13.clone.1 | convolution fusion | flops 805306368 | bytes 3277824 | tf_op jit(solution)/shard_map/vmap()/while/body/eval_jaxpr/ktu,kuw->tw/dot_general | solution.py:15
  325.2 4.2 %gather_fusion.1 = f32[16,128,256]{2,1,0:T(8,128)} fusion(f32[1,32,128,256]{3,2,1,0:T(8,128)} %get-tuple-element.352, s32[16]{0:T(128)S(1)} %or_bitcast_fusion.5), kind=kCustom, calls=%fused_computation.1.clone.1 | custom fusion | bytes 4194432 | tf_op jit(solution)/shard_map/vmap()/while/body/eval_jaxpr/gather | solution.py:14
  329.5 3.7 %fusion.58 = f32[8,1,128,256]{3,2,1,0:T(8,128)} fusion(f32[8,1,128,256]{3,2,1,0:T(8,128)} %get-tuple-element.343, s32[]{:T(128)} %get-tuple-element.342, f32[16,128,256]{2,1,0:T(8,128)} %gather_fusion.1, f32[8,1,16,128,128]{4,3,2,1,0:T(8,128)} %get-tuple-element.350), kind=kOutput, calls=%fused_computation.13.clone.1 | convolution fusion | flops 805306368 | bytes 3277824 | tf_op jit(solution)/shard_map/vmap()/while/body/eval_jaxpr/ktu,kuw->tw/dot_general | solution.py:15
  333.8 4.2 %gather_fusion.1 = f32[16,128,256]{2,1,0:T(8,128)} fusion(f32[1,32,128,256]{3,2,1,0:T(8,128)} %get-tuple-element.352, s32[16]{0:T(128)S(1)} %or_bitcast_fusion.5), kind=kCustom, calls=%fused_computation.1.clone.1 | custom fusion | bytes 4194432 | tf_op jit(solution)/shard_map/vmap()/while/body/eval_jaxpr/gather | solution.py:14
  338.1 3.7 %fusion.58 = f32[8,1,128,256]{3,2,1,0:T(8,128)} fusion(f32[8,1,128,256]{3,2,1,0:T(8,128)} %get-tuple-element.343, s32[]{:T(128)} %get-tuple-element.342, f32[16,128,256]{2,1,0:T(8,128)} %gather_fusion.1, f32[8,1,16,128,128]{4,3,2,1,0:T(8,128)} %get-tuple-element.350), kind=kOutput, calls=%fused_computation.13.clone.1 | convolution fusion | flops 805306368 | bytes 3277824 | tf_op jit(solution)/shard_map/vmap()/while/body/eval_jaxpr/ktu,kuw->tw/dot_general | solution.py:15
  342.4 4.2 %gather_fusion.1 = f32[16,128,256]{2,1,0:T(8,128)} fusion(f32[1,32,128,256]{3,2,1,0:T(8,128)} %get-tuple-element.352, s32[16]{0:T(128)S(1)} %or_bitcast_fusion.5), kind=kCustom, calls=%fused_computation.1.clone.1 | custom fusion | bytes 4194432 | tf_op jit(solution)/shard_map/vmap()/while/body/eval_jaxpr/gather | solution.py:14
  346.7 3.7 %fusion.58 = f32[8,1,128,256]{3,2,1,0:T(8,128)} fusion(f32[8,1,128,256]{3,2,1,0:T(8,128)} %get-tuple-element.343, s32[]{:T(128)} %get-tuple-element.342, f32[16,128,256]{2,1,0:T(8,128)} %gather_fusion.1, f32[8,1,16,128,128]{4,3,2,1,0:T(8,128)} %get-tuple-element.350), kind=kOutput, calls=%fused_computation.13.clone.1 | convolution fusion | flops 805306368 | bytes 3277824 | tf_op jit(solution)/shard_map/vmap()/while/body/eval_jaxpr/ktu,kuw->tw/dot_general | solution.py:15
  351.9 2.0 convolution_bitcast_fusion.2
  (88 shorter events, 34.2 us)
Async XLA Ops:
  6.5 1.6 copy-start
  6.5 60.9 %all-gather.6.cloned.1.call-start = ((), (), s32[]{:S(2)}) async-start(), calls=%async_computation.3 | async-start | bytes 5242880 | tf_op jit(solution)/shard_map/all_gather | solution.py:48
  68.5 68.9 %copy-start.2 = (f32[1024,256]{1,0:T(8,128)S(1)}, f32[1024,256]{1,0:T(8,128)}, u32[]{:S(2)}) copy-start(f32[1024,256]{1,0:T(8,128)} %fusion.28) | copy-start | bytes 3145732
  140.9 31.2 %all-to-all-start = ((f32[1,1024,256]{2,0,1:T(1,128)}), f32[1,1024,256]{2,0,1:T(1,128)S(1)}, u32[]{:S(2)}, u32[]{:S(2)}) async-start(f32[1,1024,256]{2,0,1:T(1,128)} %copy.12), calls=%async_computation | async-start | bytes 2097152 | tf_op jit(solution)/shard_map/all_to_all | solution.py:50
  145.5 134.9 %all-gather.4.cloned.1.call-start = ((), (), s32[]{:S(2)}) async-start(), calls=%async_computation.2 | async-start | bytes 5242880 | tf_op jit(solution)/shard_map/all_gather | solution.py:54
  172.0 1.2 copy-start.4
  173.3 5.0 %copy-start.1 = (f32[256,1024]{1,0:T(8,128)S(1)}, f32[256,1024]{1,0:T(8,128)}, u32[]{:S(2)}) copy-start(f32[256,1024]{1,0:T(8,128)} %param.19) | copy-start | bytes 3145732
  173.3 5.0 %copy-start.6 = (f32[1024]{0:T(1024)S(1)}, f32[1024]{0:T(1024)}, u32[]{:S(2)}) copy-start(f32[1024]{0:T(1024)} %param.20) | copy-start | bytes 12292
  281.5 68.9 %copy-start.3 = (f32[8,128,256]{2,1,0:T(8,128)S(1)}, f32[8,128,256]{2,1,0:T(8,128)}, u32[]{:S(2)}) copy-start(f32[8,128,256]{2,1,0:T(8,128)} %all_to_all.27) | copy-start | bytes 3145732
  350.4 1.5 copy-start.5
Sparse Core Ops, SparseCore 0:
  12.1 55.2 all-gather.5
  229.9 50.5 all-gather.3
where the time goes:
time: 362 us; the launch traced here: 361 us
  waiting for transfers between devices  129 us (36%)
  matrix products  84 us (23%)
  local copies, waits for them, and re-layouts  74.7 us (21%)
  blocking collectives  30.8 us (9%)
  other arithmetic  24.3 us (7%)
  between operations  13.5 us (4%)
  starting transfers between devices  4.64 us (1%)
    gather x32, local copies, waits for them, and re-layouts, row_block(): picked = blocks[ids_here]  67.7 us
    dot_general x16, matrix products, row_block(): jnp.einsum('ktu,kuw->tw', tiles_here, picked, precision=lax.Precision.HIG...  59.2 us
    all_gather x1, waiting for transfers between devices, on_device(): whole = lax.all_gather(projected, 'vtx', axis=1, tiled=True)  51.4 us
    all_gather x1, waiting for transfers between devices, on_device(): whole_two = lax.all_gather(returned, 'vtx', axis=1, tiled=True)  50.7 us
    all_to_all x1, blocking collectives, on_device(): lax.all_to_all(states, 'snap', split_axis=0, concat_axis=1, tiled=True)  30.8 us
    all_to_all x1, waiting for transfers between devices, on_device(): lax.all_to_all(hidden_one, 'snap', split_axis=1, concat_axis=0, tiled=True)  26.5 us
    dot_general x8, matrix products, advance(): jnp.dot(state_h, w_recur, precision=lax.Precision.HIGHEST)  14.1 us
    select_n x16, other arithmetic, row_block(): picked = blocks[ids_here]  10.7 us
  transfers between devices with their start and end apart: 3, of which 3 were waited for; matrix products, arithmetic and copies ran while one was open for 1% of the time, Pallas kernels for 0%

commit v1 on v0

v1 whole, which is shorter than its diff:
```python
import functools

import jax
import jax.numpy as jnp
from jax import lax
from jax.experimental import pallas as pl
from jax.experimental.pallas import tpu as pltpu
from jax.sharding import PartitionSpec as P


F32 = jnp.float32
BF16 = jnp.bfloat16
VMEM = pltpu.VMEM


def split(x):
    high = x.astype(BF16)
    return high, (x - high.astype(F32)).astype(BF16)


def mm(a, b):
    return jnp.dot(a, b, preferred_element_type=F32)


def params(mib):
    return pltpu.CompilerParams(vmem_limit_bytes=mib << 20)


def cost(flops, moved):
    return pl.CostEstimate(flops=int(flops), bytes_accessed=int(moved), transcendentals=0)


def whole():
    return pl.BlockSpec(memory_space=VMEM)


def project_kernel(x_ref, w_ref, *outs):
    wh, wl = split(w_ref[...])
    n = outs[0].shape[1]
    rows = outs[0].shape[0]
    block = min(rows, 256)
    for t in range(2):
        for b in range(0, rows, block):
            xh, xl = split(x_ref[t * rows + b : t * rows + b + block])
            y = mm(xh, wh) + mm(xl, wh) + mm(xh, wl)
            for q in range(len(outs) // 2):
                outs[2 * q + t][b : b + block] = y[:, q * n : (q + 1) * n]


def project(x, w, chunks):
    rows, depth = x.shape
    width = w.shape[1]
    n = width // chunks
    outs = pl.pallas_call(
        project_kernel,
        in_specs=[whole()] * 2,
        out_specs=[whole()] * (2 * chunks),
        out_shape=[jax.ShapeDtypeStruct((rows // 2, n), F32)] * (2 * chunks),
        compiler_params=params(12),
        cost_estimate=cost(6 * rows * depth * width, 4 * rows * (depth + width)),
        name="project",
    )(x, w)
    return [outs[2 * q : 2 * q + 2] for q in range(chunks)]


def prepare_kernel(t_ref, a_ref, s_ref):
    _, kt, tile, _ = t_ref.shape
    total = jnp.zeros((tile, tile), F32)
    for k in range(kt):
        t = t_ref[0, k]
        total = total + t * t
        high, low = split(t)
        a_ref[0, :tile, k * tile : (k + 1) * tile] = high
        a_ref[0, tile:, k * tile : (k + 1) * tile] = low
    s = lax.rsqrt(1.0 + jnp.sum(total, axis=1, keepdims=True))
    s_ref[0] = jnp.broadcast_to(s, (tile, tile))


def prepare(tiles):
    nb, kt, tile, _ = tiles.shape
    return pl.pallas_call(
        prepare_kernel,
        grid=(nb,),
        in_specs=[pl.BlockSpec((1, kt, tile, tile), lambda i: (i, 0, 0, 0))],
        out_specs=[
            pl.BlockSpec((1, 2 * tile, kt * tile), lambda i: (i, 0, 0)),
            pl.BlockSpec((1, tile, tile), lambda i: (i, 0, 0)),
        ],
        out_shape=[
            jax.ShapeDtypeStruct((nb, 2 * tile, kt * tile), BF16),
            jax.ShapeDtypeStruct((nb, tile, tile), F32),
        ],
        compiler_params=params(12),
        cost_estimate=cost(8 * tiles.size, 8 * tiles.size),
        name="prepare",
    )(tiles)


def weights_kernel(wi_ref, wr_ref, wo_ref, wih, wil, weh, wel):
    wih[...], wil[...] = split(wi_ref[...])
    n = wr_ref.shape[1]
    weh[:, :n], wel[:, :n] = split(wr_ref[...])
    weh[:, n:], wel[:, n:] = split(wo_ref[...])


def split_weights(w_input, w_recur, w_second):
    wide = (w_recur.shape[0], w_recur.shape[1] + w_second.shape[1])
    return pl.pallas_call(
        weights_kernel,
        in_specs=[whole()] * 3,
        out_specs=[whole()] * 4,
        out_shape=[jax.ShapeDtypeStruct(shape, BF16) for shape in (w_input.shape, w_input.shape, wide, wide)],
        compiler_params=params(12),
        cost_estimate=cost(1, 16 * w_input.size),
        name="split_weights",
    )(w_input, w_recur, w_second)


def place_of(source, slab):
    flipped, number, _ = source
    return slab ^ number if flipped else number


def conv_one_kernel(sources, sub, blocks, cols, a_ref, s_ref, *rest):
    if sources is None:
        y, own, outs, hold = rest[0], rest[1], rest[2:-1], rest[-1]
    else:
        refs, outs, y, own, hold = rest[: len(sources)], rest[len(sources) : -3], *rest[-3:]
    _, tile, _ = s_ref.shape
    rows, n = own.shape
    snap, slab = lax.axis_index("snap"), lax.axis_index("vtx")
    per = tile // sub
    for source, ref in zip(sources or (), refs if sources else ()):
        start = place_of(source, slab) * rows + source[2]
        for b in range(0, ref.shape[0], tile):
            value = ref[b : b + tile]
            where = pl.ds(pl.multiple_of(start + b, tile), tile)
            y[where, :n], y[where, n:] = split(value)
            if source[:2] == (True, 0):
                own[source[2] + b : source[2] + b + tile] = value

    @pl.loop(*blocks)
    def _(q):
        r = q ^ (snap // per)
        kt = cols.shape[1]
        rhs = jnp.concatenate([y[pl.ds(pl.multiple_of(cols[r, k] * tile, tile), tile), :] for k in range(kt)], axis=0)
        acc = mm(a_ref[r, :tile, :], rhs)
        low = mm(a_ref[r, tile:, :], rhs[:, :n])
        mine = own[pl.ds(pl.multiple_of(r * tile, tile), tile), :]
        hidden = jnp.maximum(s_ref[r][:, :n] * (mine + acc[:, :n] + acc[:, n:] + low), 0.0)
        for i in range(per):
            hold[(r * per + i) ^ snap] = hidden[i * sub : (i + 1) * sub]

    for i, out in enumerate(outs):
        out[...] = hold[blocks[0] * per + i]


def conv_one(cols, a, s, sources, arrays, n_snap, rows, verts, blocks, keep=False):
    nb, two, deep = a.shape
    n = arrays[1].shape[-1]
    sub = rows // n_snap
    per = two // 2 // sub
    count = (blocks[1] - blocks[0]) * per
    smem = pl.BlockSpec(memory_space=pltpu.SMEM)
    hold = VMEM((n_snap, sub, n), F32)
    outs = [jax.ShapeDtypeStruct((sub, n), F32)] * count
    held = [jax.ShapeDtypeStruct((verts, 2 * n), BF16), jax.ShapeDtypeStruct((rows, n), F32)]
    scratch = [hold]
    if keep:
        outs = outs + held
    elif sources is not None:
        scratch = [VMEM(h.shape, h.dtype) for h in held] + scratch
    return pl.pallas_call(
        functools.partial(conv_one_kernel, sources and tuple(sources), sub, blocks),
        in_specs=[smem] + [whole()] * (2 + len(arrays)),
        out_specs=[whole()] * len(outs),
        scratch_shapes=scratch,
        out_shape=outs,
        compiler_params=params(20),
        cost_estimate=cost(2 * nb * two * deep * 2 * n, 2 * a.size + 4 * verts * n),
        name="conv_one",
    )(cols, a, s, *arrays)


def sigmoid(x):
    return 0.5 * jnp.tanh(0.5 * x) + 0.5


def lstm_kernel(n_snap, chunks, *refs):
    pieces = refs[: n_snap * chunks]
    wih, wil, weh, wel, bias = refs[n_snap * chunks : n_snap * chunks + 5]
    outs = refs[n_snap * chunks + 5 : -3]
    xh, xl, done = refs[-3:]
    snap = lax.axis_index("snap")
    sub, n = pieces[0].shape
    width = n * chunks
    wide = 4 * width
    for q in range(chunks):
        for i in range(n_snap):
            high, low = split(pieces[q * n_snap + i][...])
            where = pl.ds(pl.multiple_of((snap ^ i) * sub, sub), sub)
            xh[where, q * n : (q + 1) * n] = high
            xl[where, q * n : (q + 1) * n] = low

    def fresh(s):
        at = slice(s * sub, (s + 1) * sub)
        both = mm(jnp.concatenate([xh[at], xl[at]], axis=0), wih[...])
        return both[:sub] + both[sub:] + mm(xh[at], wil[...]) + bias[...]

    c = recur = None
    following = fresh(0)
    for s in range(n_snap):
        at = slice(s * sub, (s + 1) * sub)
        gates = following if recur is None else following + recur
        following = fresh(s + 1) if s < n_snap - 1 else None
        gi, gf, gg, go = (gates[:, i * width : (i + 1) * width] for i in range(4))
        new = sigmoid(gi) * jnp.tanh(gg)
        c = new if c is None else sigmoid(gf) * c + new
        high, low = split(sigmoid(go) * jnp.tanh(c))
        first = 0 if s < n_snap - 1 else wide
        both = mm(jnp.concatenate([high, low], axis=0), weh[:, first:])
        both = both[:sub] + both[sub:] + mm(high, wel[:, first:])
        recur = both[:, :wide]
        done[at] = both[:, wide - first :]
    for i, out in enumerate(outs):
        out[...] = done[pl.ds(pl.multiple_of((i ^ snap) * sub, sub), sub), :]


def lstm(pieces, weights, bias, n_snap, chunks):
    sub, n = pieces[0].shape
    width = n * chunks
    return pl.pallas_call(
        functools.partial(lstm_kernel, n_snap, chunks),
        in_specs=[whole()] * (len(pieces) + 5),
        out_specs=[whole()] * n_snap,
        out_shape=[jax.ShapeDtypeStruct((sub, width), F32)] * n_snap,
        scratch_shapes=[VMEM((n_snap * sub, width), BF16)] * 2 + [VMEM((n_snap * sub, width), F32)],
        compiler_params=params(20),
        cost_estimate=cost(12 * n_snap * sub * width * 4 * width, 8 * n_snap * sub * width),
        name="lstm",
    )(*pieces, *weights, bias)


def conv_two_kernel(sources, cols, a_ref, s_ref, *rest):
    refs, out_ref, (yh, yl, own, ready, sems) = rest[: len(sources)], rest[len(sources)], rest[len(sources) + 1 :]
    nb, tile, _ = s_ref.shape
    rows = own.shape[0]
    snap, slab = lax.axis_index("snap"), lax.axis_index("vtx")
    for source, ref in zip(sources, refs):
        sub = ref.shape[0]
        at = (source[2] ^ snap) * sub
        where = pl.ds(pl.multiple_of(place_of(source, slab) * rows + at, sub), sub)
        value = ref[...]
        yh[where, :], yl[where, :] = split(value)
        if source[:2] == (True, 0):
            own[pl.ds(pl.multiple_of(at, sub), sub), :] = value

    def leave(r):
        where = pl.ds(pl.multiple_of(r * tile, tile), tile)
        return pltpu.make_async_copy(ready.at[where, :], out_ref.at[where, :], sems.at[r])

    @pl.loop(0, nb)
    def _(r):
        kt = cols.shape[1]
        at = [pl.ds(pl.multiple_of(cols[r, k] * tile, tile), tile) for k in range(kt)]
        high = jnp.concatenate([yh[w, :] for w in at], axis=0)
        low = jnp.concatenate([yl[w, :] for w in at], axis=0)
        ah, al = a_ref[r, :tile, :], a_ref[r, tile:, :]
        where = pl.ds(pl.multiple_of(r * tile, tile), tile)
        ready[where, :] = s_ref[r][:, :1] * (own[where, :] + (mm(ah, high) + mm(al, high) + mm(ah, low)))
        leave(r).start()

    for r in range(nb):
        leave(r).wait()


def conv_two(cols, a, s, sources, arrays, rows, verts):
    nb, two, deep = a.shape
    width = arrays[0].shape[-1]
    smem = pl.BlockSpec(memory_space=pltpu.SMEM)
    return pl.pallas_call(
        functools.partial(conv_two_kernel, tuple(sources)),
        in_specs=[smem] + [whole()] * (2 + len(arrays)),
        out_specs=pl.BlockSpec(memory_space=pltpu.HBM),
        scratch_shapes=[VMEM((verts, width), BF16)] * 2
        + [VMEM((rows, width), F32)] * 2
        + [pltpu.SemaphoreType.DMA((nb,))],
        out_shape=jax.ShapeDtypeStruct((rows, width), F32),
        compiler_params=params(24),
        cost_estimate=cost(3 * nb * two * deep * width, 2 * a.size + 4 * verts * width),
        name="conv_two",
    )(cols, a, s, *arrays)


def hop(x, axis, bits, size):
    return lax.ppermute(x, axis, [(i, i ^ bits) for i in range(size)])


def gather(x, n_vtx, at, by_x):
    if n_vtx != 4:
        every = lax.all_gather(x, "vtx", axis=0)
        return [(True, 0, at)] + [(False, v, at) for v in range(n_vtx)], [x] + [every[v] for v in range(n_vtx)]
    from_x = hop(x, "vtx", 1, n_vtx)
    from_y = hop(x, "vtx", 2, n_vtx)
    cross = hop(from_y, "vtx", 1, n_vtx) if by_x else hop(from_x, "vtx", 2, n_vtx)
    return [(True, m, at) for m in range(4)], [x, from_x, from_y, cross]


def exchange(pieces, n_snap):
    return [p if i == 0 else hop(p, "snap", i, n_snap) for i, p in enumerate(pieces)]


def on_device(n_snap, n_vtx, feats, col_ids, tiles, w_first, w_input, w_recur, lstm_bias, w_second):
    x, cols = feats[0], col_ids[0]
    rows = x.shape[0]
    verts = rows * n_vtx
    half = rows // 2
    nb = cols.shape[0]
    projected = project(x, w_first, 2)
    a, s = prepare(tiles[0])
    weights = split_weights(w_input, w_recur, w_second)
    pieces = []
    for name, own in zip("ab", projected):
        sources, arrays = [], []
        for t in range(2):
            more = gather(own[t], n_vtx, t * half, t == 1)
            sources += more[0]
            arrays += more[1]
        near, far = (0, nb // 2), (nb // 2, nb)
        if name == "a":
            hidden = conv_one(cols, a, s, sources, arrays, n_snap, rows, verts, (0, nb))
        else:
            *distant, y, kept = conv_one(cols, a, s, sources, arrays, n_snap, rows, verts, far, True)
        if name == "b":
            hidden = [*conv_one(cols, a, s, None, [y, kept], n_snap, rows, verts, near), *distant]
        pieces += exchange(hidden, n_snap)
    states = lstm(pieces, weights, lstm_bias[None], n_snap, 2)
    sources, arrays = [], []
    for i, piece in enumerate(exchange(states, n_snap)):
        more = gather(piece, n_vtx, i, i % 2 == 1)
        sources += more[0]
        arrays += more[1]
    out = conv_two(cols, a, s, sources, arrays, rows, verts)
    return out[None]


def solution(mesh):
    placed = (
        P("snap", "vtx", None),
        P("snap", "vtx", None),
        P("snap", "vtx", None, None, None),
        P(),
        P(),
        P(),
        P(),
        P(),
    )
    n_snap, n_vtx = mesh.shape["snap"], mesh.shape["vtx"]
    body = functools.partial(on_device, n_snap, n_vtx)
    return jax.shard_map(body, mesh=mesh, in_specs=placed, out_specs=P("snap", "vtx", None), check_vma=False)
```

time: 362 us -> 144 us (0.40)
  waiting for transfers between devices: 129 us -> 39.5 us
  matrix products: 84 us -> 0 us
  local copies, waits for them, and re-layouts: 74.7 us -> 6.06 us
  starting transfers between devices: 4.64 us -> 72.5 us
  blocking collectives: 30.8 us -> 0 us
  Pallas kernels: 0 us -> 25.4 us
  other arithmetic: 24.3 us -> 0 us
  between operations: 13.5 us -> 0.21 us
    all_gather x2 -> x0, waiting for transfers between devices: 102 us -> none  [the longest x1 51.4 us: on_device(): whole = lax.all_gather(projected, 'vtx', axis=1, tiled=True)]
    dot_general x27 -> x0, matrix products: 84 us -> none  [the longest x16 59.2 us: row_block(): jnp.einsum('ktu,kuw->tw', tiles_here, picked, precision=lax.Precision.HIG...]
    ppermute x0 -> x57, starting transfers between devices: none -> 72.5 us  [hop(): return lax.ppermute(x, axis, [(i, i ^ bits) for i in range(size)])]
    gather x32 -> x0, local copies, waits for them, and re-layouts: 67.7 us -> none  [row_block(): picked = blocks[ids_here]]
    ppermute x0 -> x57, waiting for transfers between devices: none -> 39.5 us  [hop(): return lax.ppermute(x, axis, [(i, i ^ bits) for i in range(size)])]
    all_to_all x1 -> x0, blocking collectives: 30.8 us -> none  [on_device(): lax.all_to_all(states, 'snap', split_axis=0, concat_axis=1, tiled=True)]
    all_to_all x1 -> x0, waiting for transfers between devices: 26.5 us -> none  [on_device(): lax.all_to_all(hidden_one, 'snap', split_axis=1, concat_axis=0, tiled=True)]
    pallas_call x0 -> x8, Pallas kernels: none -> 25.4 us  [the longest x3 9.7 us: conv_one(): pl.pallas_call(functools.partial(conv_one_kernel, sources and tuple(sourc...]
  transfers between devices with their start and end apart: 3 -> 57, of which waited for: 3 -> 14; matrix products, arithmetic and copies ran while one was open for 1% -> 0% of each run, Pallas kernels for 0% -> 9%
where the time goes in v1:
time: 144 us
  starting transfers between devices  72.5 us (50%)
  waiting for transfers between devices  39.5 us (27%)
  Pallas kernels  25.4 us (18%)
  local copies, waits for them, and re-layouts  6.06 us (4%)
    ppermute x57, starting transfers between devices, hop(): return lax.ppermute(x, axis, [(i, i ^ bits) for i in range(size)])  72.5 us
    ppermute x57, waiting for transfers between devices, hop(): return lax.ppermute(x, axis, [(i, i ^ bits) for i in range(size)])  39.5 us
    pallas_call x3, Pallas kernels, conv_one(): pl.pallas_call(functools.partial(conv_one_kernel, sources and tuple(sourc...  9.7 us
    pallas_call x1, Pallas kernels, conv_two(): pl.pallas_call(functools.partial(conv_two_kernel, tuple(sources)), in_spe...  6.8 us
    unnamed x16, local copies, waits for them, and re-layouts  6.06 us
    pallas_call x1, Pallas kernels, lstm(): pl.pallas_call(functools.partial(lstm_kernel, n_snap, chunks), in_specs=[...  4.58 us
    pallas_call x1, Pallas kernels, prepare(): pl.pallas_call(prepare_kernel, grid=(nb,), in_specs=[pl.BlockSpec((1, kt,...  2.92 us
  transfers between devices with their start and end apart: 57, of which 14 were waited for; matrix products, arithmetic and copies ran while one was open for 0% of the time, Pallas kernels for 9%

profile of v1, /device:TPU:0, one launch (start us, length us, event | category | flops | bytes accessed | tf_op | source)
XLA Modules:
  0.0 143.7 jit_solution(17847780137018145034)
XLA Ops:
  0.0 1.6 %copy-done.5 = f32[1,1024,512]{2,1,0:T(8,128)S(1)} copy-done((f32[1,1024,512]{2,1,0:T(8,128)S(1)}, f32[1,1024,512]{2,1,0:T(8,128)}, u32[]{:S(2)}) %copy-start.5) | copy-done | bytes 2097176
  3.7 3.0 %collective-permute-start = (f32[512,128]{1,0:T(8,128)S(1)}, f32[512,128]{1,0:T(8,128)S(1)}, u32[]{:S(2)}, u32[]{:S(2)}) collective-permute-start(f32[512,128]{1,0:T(8,128)S(1)} %get-tuple-element.43.rest_0_), channel_id=1, source_target_pairs={{0,1},{1,0},{2,3},{3,2},{4,5},{5,4},{6,7},{7,6},{8,9},{9,8},{10,11... | collective-permute-start | bytes 786440 | tf_op jit(solution)/shard_map/ppermute | solution.py:296
  6.7 1.5 %collective-permute-start.1 = (f32[512,128]{1,0:T(8,128)S(1)}, f32[512,128]{1,0:T(8,128)S(1)}, u32[]{:S(2)}, u32[]{:S(2)}) collective-permute-start(f32[512,128]{1,0:T(8,128)S(1)} %get-tuple-element.43.rest_0_), channel_id=1, source_target_pairs={{0,2},{1,3},{2,0},{3,1},{4,6},{5,7},{6,4},{7,5},{8,10},{9,11},{10,... | collective-permute-start | bytes 786440 | tf_op jit(solution)/shard_map/ppermute | solution.py:296
  8.8 1.9 %collective-permute-start.13 = (f32[512,128]{1,0:T(8,128)S(1)}, f32[512,128]{1,0:T(8,128)S(1)}, u32[]{:S(2)}, u32[]{:S(2)}) collective-permute-start(f32[512,128]{1,0:T(8,128)S(1)} %get-tuple-element.53.rest_0_), channel_id=1, source_target_pairs={{0,1},{1,0},{2,3},{3,2},{4,5},{5,4},{6,7},{7,6},{8,9},{9,8},{10,11... | collective-permute-start | bytes 786440 | tf_op jit(solution)/shard_map/ppermute | solution.py:296
  10.8 3.1 %collective-permute-done.rest_1_ = f32[512,128]{1,0:T(8,128)S(1)} collective-permute-done((f32[512,128]{1,0:T(8,128)S(1)}, f32[512,128]{1,0:T(8,128)S(1)}, u32[]{:S(2)}, u32[]{:S(2)}) %collective-permute-start) | collective-permute-done | bytes 262176 | tf_op jit(solution)/shard_map/ppermute | solution.py:296
  13.9 2.1 %collective-permute-start.17 = (f32[512,128]{1,0:T(8,128)S(1)}, f32[512,128]{1,0:T(8,128)S(1)}, u32[]{:S(2)}, u32[]{:S(2)}) collective-permute-start(f32[512,128]{1,0:T(8,128)S(1)} %get-tuple-element.54.rest_4_), channel_id=1, source_target_pairs={{0,2},{1,3},{2,0},{3,1},{4,6},{5,7},{6,4},{7,5},{8,10},{9,11},{10,... | collective-permute-start | bytes 786440 | tf_op jit(solution)/shard_map/ppermute | solution.py:296
  15.9 1.5 %collective-permute-start.2 = (f32[512,128]{1,0:T(8,128)S(1)}, f32[512,128]{1,0:T(8,128)S(1)}, u32[]{:S(2)}, u32[]{:S(2)}) collective-permute-start(f32[512,128]{1,0:T(8,128)S(1)} %collective-permute-done.rest_1_), channel_id=1, source_target_pairs={{0,2},{1,3},{2,0},{3,1},{4,6},{5,7},{6,4},{7,5},{8,10},{9,11},{10,... | collective-permute-start | bytes 786440 | tf_op jit(solution)/shard_map/ppermute | solution.py:296
  17.4 4.1 %collective-permute-done.4.rest_6_ = f32[512,128]{1,0:T(8,128)S(1)} collective-permute-done((f32[512,128]{1,0:T(8,128)S(1)}, f32[512,128]{1,0:T(8,128)S(1)}, u32[]{:S(2)}, u32[]{:S(2)}) %collective-permute-start.4) | collective-permute-done | bytes 262176 | tf_op jit(solution)/shard_map/ppermute | solution.py:296
  21.6 2.0 %collective-permute-start.14 = (f32[512,128]{1,0:T(8,128)S(1)}, f32[512,128]{1,0:T(8,128)S(1)}, u32[]{:S(2)}, u32[]{:S(2)}) collective-permute-start(f32[512,128]{1,0:T(8,128)S(1)} %get-tuple-element.53.rest_0_), channel_id=1, source_target_pairs={{0,2},{1,3},{2,0},{3,1},{4,6},{5,7},{6,4},{7,5},{8,10},{9,11},{10,... | collective-permute-start | bytes 786440 | tf_op jit(solution)/shard_map/ppermute | solution.py:296
  23.6 1.5 %collective-permute-done.13.rest_1_ = f32[512,128]{1,0:T(8,128)S(1)} collective-permute-done((f32[512,128]{1,0:T(8,128)S(1)}, f32[512,128]{1,0:T(8,128)S(1)}, u32[]{:S(2)}, u32[]{:S(2)}) %collective-permute-start.13) | collective-permute-done | bytes 262176 | tf_op jit(solution)/shard_map/ppermute | solution.py:296
  25.1 2.0 %collective-permute-start.16 = (f32[512,128]{1,0:T(8,128)S(1)}, f32[512,128]{1,0:T(8,128)S(1)}, u32[]{:S(2)}, u32[]{:S(2)}) collective-permute-start(f32[512,128]{1,0:T(8,128)S(1)} %get-tuple-element.54.rest_4_), channel_id=1, source_target_pairs={{0,1},{1,0},{2,3},{3,2},{4,5},{5,4},{6,7},{7,6},{8,9},{9,8},{10,11... | collective-permute-start | bytes 786440 | tf_op jit(solution)/shard_map/ppermute | solution.py:296
  27.1 1.5 %collective-permute-start.15 = (f32[512,128]{1,0:T(8,128)S(1)}, f32[512,128]{1,0:T(8,128)S(1)}, u32[]{:S(2)}, u32[]{:S(2)}) collective-permute-start(f32[512,128]{1,0:T(8,128)S(1)} %collective-permute-done.13.rest_1_), channel_id=1, source_target_pairs={{0,2},{1,3},{2,0},{3,1},{4,6},{5,7},{6,4},{7,5},{8,10},{9,11},{10,... | collective-permute-start | bytes 786440 | tf_op jit(solution)/shard_map/ppermute | solution.py:296
  28.6 4.1 %collective-permute-done.2.rest_3_ = f32[512,128]{1,0:T(8,128)S(1)} collective-permute-done((f32[512,128]{1,0:T(8,128)S(1)}, f32[512,128]{1,0:T(8,128)S(1)}, u32[]{:S(2)}, u32[]{:S(2)}) %collective-permute-start.2) | collective-permute-done | bytes 262176 | tf_op jit(solution)/shard_map/ppermute | solution.py:296
  32.8 3.4 %copy-done = f32[1,8,16,128,128]{4,3,2,1,0:T(8,128)S(1)} copy-done((f32[1,8,16,128,128]{4,3,2,1,0:T(8,128)S(1)}, f32[1,8,16,128,128]{4,3,2,1,0:T(8,128)}, u32[]{:S(2)}) %copy-start) | copy-done | bytes 8388632
  36.2 2.9 %prepare.1 = (bf16[8,256,2048]{2,1,0:T(8,128)(2,1)S(1)}, f32[8,128,128]{2,1,0:T(8,128)S(1)}) custom-call(f32[8,16,128,128]{3,2,1,0:T(8,128)S(1)} %bitcast.5), custom_call_target="tpu_custom_call" | custom-call | flops 16777216 | bytes 16777216 | tf_op jit(solution)/shard_map/prepare/pallas_call | solution.py:81
  39.1 4.6 %conv_one.3 = (f32[128,128]{1,0:T(8,128)S(1)}, f32[128,128]{1,0:T(8,128)S(1)}, f32[128,128]{1,0:T(8,128)S(1)}, f32[128,128]{1,0:T(8,128)S(1)}, f32[128,128]{1,0:...) custom-call(s32[8,16]{1,0:T(8,128)S(1)} %bitcast.6, ...), custom_call_target="tpu_custom_call" | custom-call | flops 2147483648 | bytes 10485760 | tf_op jit(solution)/shard_map/conv_one/pallas_call | solution.py:173
  43.8 2.1 %collective-permute-start.7 = (f32[128,128]{1,0:T(8,128)S(1)}, f32[128,128]{1,0:T(8,128)S(1)}, u32[]{:S(2)}, u32[]{:S(2)}) collective-permute-start(f32[128,128]{1,0:T(8,128)S(1)} %get-tuple-element.47), channel_id=1, source_target_pairs={{0,8},{4,12},{8,0},{12,4},{16,24},{20,28},{24,16},{28,20},{1,9},{5... | collective-permute-start | bytes 196616 | tf_op jit(solution)/shard_map/ppermute | solution.py:296
  46.0 2.7 %collective-permute-start.9 = (f32[128,128]{1,0:T(8,128)S(1)}, f32[128,128]{1,0:T(8,128)S(1)}, u32[]{:S(2)}, u32[]{:S(2)}) collective-permute-start(f32[128,128]{1,0:T(8,128)S(1)} %get-tuple-element.49), channel_id=1, source_target_pairs={{0,16},{4,20},{8,24},{12,28},{16,0},{20,4},{24,8},{28,12},{1,17},{... | collective-permute-start | bytes 196616 | tf_op jit(solution)/shard_map/ppermute | solution.py:296
  48.7 2.7 %conv_one.4 = (f32[128,128]{1,0:T(8,128)S(1)}, f32[128,128]{1,0:T(8,128)S(1)}, f32[128,128]{1,0:T(8,128)S(1)}, f32[128,128]{1,0:T(8,128)S(1)}, bf16[4096,256]{1,0:T(8,128)(2,1)S(1)}, /*index=5*/f32[1024,128]{1,0:T(8,128)S(1)}) custom-call(s32[8,16]{1,0:T(8,128)S(1)} %bitcast.7, bf16[8,256,2048]{2,1,0:T(8,128)(2,1)S(1)} %get-tuple-element.41.a_ref, ...), custom_call_target="tpu_custom_call" | custom-call | flops 2147483648 | bytes 10485760 | tf_op jit(solution)/shard_map/conv_one/pallas_call | solution.py:173
  51.5 2.4 %conv_one.5 = (f32[128,128]{1,0:T(8,128)S(1)}, f32[128,128]{1,0:T(8,128)S(1)}, f32[128,128]{1,0:T(8,128)S(1)}, f32[128,128]{1,0:T(8,128)S(1)}) custom-call(s32[8,16]{1,0:T(8,128)S(1)} %bitcast.8, bf16[8,256,2048]{2,1,0:T(8,128)(2,1)S(1)} %get-tuple-element.41.a_ref, f32[8,128,128]{2,1,0:T(8,128)S(1)} %get-tuple-element.42.s_ref, ...), custom_call_target="tpu_custom_call" | custom-call | flops 2147483648 | bytes 10485760 | tf_op jit(solution)/shard_map/conv_one/pallas_call | solution.py:173
  53.9 3.7 %collective-permute-start.11 = (f32[128,128]{1,0:T(8,128)S(1)}, f32[128,128]{1,0:T(8,128)S(1)}, u32[]{:S(2)}, u32[]{:S(2)}) collective-permute-start(f32[128,128]{1,0:T(8,128)S(1)} %get-tuple-element.51), channel_id=1, source_target_pairs={{0,24},{4,28},{8,16},{12,20},{16,8},{20,12},{24,0},{28,4},{1,25},{... | collective-permute-start | bytes 196616 | tf_op jit(solution)/shard_map/ppermute | solution.py:296
  58.0 1.6 %collective-permute-start.21 = (f32[128,128]{1,0:T(8,128)S(1)}, f32[128,128]{1,0:T(8,128)S(1)}, u32[]{:S(2)}, u32[]{:S(2)}) collective-permute-start(f32[128,128]{1,0:T(8,128)S(1)} %get-tuple-element.60), channel_id=1, source_target_pairs={{0,12},{4,8},{8,4},{12,0},{16,28},{20,24},{24,20},{28,16},{1,13},{... | collective-permute-start | bytes 196616 | tf_op jit(solution)/shard_map/ppermute | solution.py:296
  60.4 1.8 %collective-permute-start.22 = (f32[128,128]{1,0:T(8,128)S(1)}, f32[128,128]{1,0:T(8,128)S(1)}, u32[]{:S(2)}, u32[]{:S(2)}) collective-permute-start(f32[128,128]{1,0:T(8,128)S(1)} %get-tuple-element.61), channel_id=1, source_target_pairs={{0,16},{4,20},{8,24},{12,28},{16,0},{20,4},{24,8},{28,12},{1,17},{... | collective-permute-start | bytes 196616 | tf_op jit(solution)/shard_map/ppermute | solution.py:296
  62.2 1.4 collective-permute-done.12.refs_7_
  63.6 1.4 collective-permute-start.23
  66.0 1.7 %collective-permute-start.25 = (f32[128,128]{1,0:T(8,128)S(1)}, f32[128,128]{1,0:T(8,128)S(1)}, u32[]{:S(2)}, u32[]{:S(2)}) collective-permute-start(f32[128,128]{1,0:T(8,128)S(1)} %get-tuple-element.64), channel_id=1, source_target_pairs={{0,28},{4,24},{8,20},{12,16},{16,12},{20,8},{24,4},{28,0},{1,29},{... | collective-permute-start | bytes 196616 | tf_op jit(solution)/shard_map/ppermute | solution.py:296
  68.1 5.5 %collective-permute-done.23.refs_13_ = f32[128,128]{1,0:T(8,128)S(1)} collective-permute-done((f32[128,128]{1,0:T(8,128)S(1)}, f32[128,128]{1,0:T(8,128)S(1)}, u32[]{:S(2)}, u32[]{:S(2)}) %collective-permute-start.23) | collective-permute-done | bytes 65568 | tf_op jit(solution)/shard_map/ppermute | solution.py:296
  73.6 4.6 %lstm.1 = (f32[128,256]{1,0:T(8,128)S(1)}, f32[128,256]{1,0:T(8,128)S(1)}, f32[128,256]{1,0:T(8,128)S(1)}, f32[128,256]{1,0:T(8,128)S(1)}, f32[128,256]{1,0:T(8,...) custom-call(f32[128,128]{1,0:T(8,128)S(1)} %get-tuple-element.45.refs_0_, ...), custom_call_target="tpu_custom_call" | custom-call | flops 3221225472 | bytes 2097152 | tf_op jit(solution)/shard_map/lstm/pallas_call | solution.py:232
  78.2 1.5 %collective-permute-start.26 = (f32[128,256]{1,0:T(8,128)S(1)}, f32[128,256]{1,0:T(8,128)S(1)}, u32[]{:S(2)}, u32[]{:S(2)}) collective-permute-start(f32[128,256]{1,0:T(8,128)S(1)} %get-tuple-element.69.rest_0_), channel_id=1, source_target_pairs={{0,1},{1,0},{2,3},{3,2},{4,5},{5,4},{6,7},{7,6},{8,9},{9,8},{10,11... | collective-permute-start | bytes 393224 | tf_op jit(solution)/shard_map/ppermute | solution.py:296
  79.7 1.5 %collective-permute-start.27 = (f32[128,256]{1,0:T(8,128)S(1)}, f32[128,256]{1,0:T(8,128)S(1)}, u32[]{:S(2)}, u32[]{:S(2)}) collective-permute-start(f32[128,256]{1,0:T(8,128)S(1)} %get-tuple-element.69.rest_0_), channel_id=1, source_target_pairs={{0,2},{1,3},{2,0},{3,1},{4,6},{5,7},{6,4},{7,5},{8,10},{9,11},{10,... | collective-permute-start | bytes 393224 | tf_op jit(solution)/shard_map/ppermute | solution.py:296
  81.2 3.4 %collective-permute-start.33 = (f32[128,256]{1,0:T(8,128)S(1)}, f32[128,256]{1,0:T(8,128)S(1)}, u32[]{:S(2)}, u32[]{:S(2)}) collective-permute-start(f32[128,256]{1,0:T(8,128)S(1)} %get-tuple-element.71), channel_id=1, source_target_pairs={{0,8},{4,12},{8,0},{12,4},{16,24},{20,28},{24,16},{28,20},{1,9},{5... | collective-permute-start | bytes 393224 | tf_op jit(solution)/shard_map/ppermute | solution.py:296
  84.7 2.9 %collective-permute-start.41 = (f32[128,256]{1,0:T(8,128)S(1)}, f32[128,256]{1,0:T(8,128)S(1)}, u32[]{:S(2)}, u32[]{:S(2)}) collective-permute-start(f32[128,256]{1,0:T(8,128)S(1)} %get-tuple-element.73), channel_id=1, source_target_pairs={{0,16},{4,20},{8,24},{12,28},{16,0},{20,4},{24,8},{28,12},{1,17},{... | collective-permute-start | bytes 393224 | tf_op jit(solution)/shard_map/ppermute | solution.py:296
  87.8 1.8 %collective-permute-start.49 = (f32[128,256]{1,0:T(8,128)S(1)}, f32[128,256]{1,0:T(8,128)S(1)}, u32[]{:S(2)}, u32[]{:S(2)}) collective-permute-start(f32[128,256]{1,0:T(8,128)S(1)} %get-tuple-element.75), channel_id=1, source_target_pairs={{0,24},{4,28},{8,16},{12,20},{16,8},{20,12},{24,0},{28,4},{1,25},{... | collective-permute-start | bytes 393224 | tf_op jit(solution)/shard_map/ppermute | solution.py:296
  89.5 3.9 %collective-permute-done.33.rest_8_ = f32[128,256]{1,0:T(8,128)S(1)} collective-permute-done((f32[128,256]{1,0:T(8,128)S(1)}, f32[128,256]{1,0:T(8,128)S(1)}, u32[]{:S(2)}, u32[]{:S(2)}) %collective-permute-start.33) | collective-permute-done | bytes 131104 | tf_op jit(solution)/shard_map/ppermute | solution.py:296
  94.4 1.5 %collective-permute-done.37.rest_12_ = f32[128,256]{1,0:T(8,128)S(1)} collective-permute-done((f32[128,256]{1,0:T(8,128)S(1)}, f32[128,256]{1,0:T(8,128)S(1)}, u32[]{:S(2)}, u32[]{:S(2)}) %collective-permute-start.37) | collective-permute-done | bytes 131104 | tf_op jit(solution)/shard_map/ppermute | solution.py:296
  96.0 9.6 %collective-permute-done.45.rest_20_ = f32[128,256]{1,0:T(8,128)S(1)} collective-permute-done((f32[128,256]{1,0:T(8,128)S(1)}, f32[128,256]{1,0:T(8,128)S(1)}, u32[]{:S(2)}, u32[]{:S(2)}) %collective-permute-start.45) | collective-permute-done | bytes 131104 | tf_op jit(solution)/shard_map/ppermute | solution.py:296
  105.5 1.5 %collective-permute-start.31 = (f32[128,256]{1,0:T(8,128)S(1)}, f32[128,256]{1,0:T(8,128)S(1)}, u32[]{:S(2)}, u32[]{:S(2)}) collective-permute-start(f32[128,256]{1,0:T(8,128)S(1)} %collective-permute-done.29.rest_4_), channel_id=1, source_target_pairs={{0,2},{1,3},{2,0},{3,1},{4,6},{5,7},{6,4},{7,5},{8,10},{9,11},{10,... | collective-permute-start | bytes 393224 | tf_op jit(solution)/shard_map/ppermute | solution.py:296
  109.6 1.5 %collective-permute-start.39 = (f32[128,256]{1,0:T(8,128)S(1)}, f32[128,256]{1,0:T(8,128)S(1)}, u32[]{:S(2)}, u32[]{:S(2)}) collective-permute-start(f32[128,256]{1,0:T(8,128)S(1)} %collective-permute-done.37.rest_12_), channel_id=1, source_target_pairs={{0,2},{1,3},{2,0},{3,1},{4,6},{5,7},{6,4},{7,5},{8,10},{9,11},{10,... | collective-permute-start | bytes 393224 | tf_op jit(solution)/shard_map/ppermute | solution.py:296
  111.0 2.3 %collective-permute-start.42 = (f32[128,256]{1,0:T(8,128)S(1)}, f32[128,256]{1,0:T(8,128)S(1)}, u32[]{:S(2)}, u32[]{:S(2)}) collective-permute-start(f32[128,256]{1,0:T(8,128)S(1)} %collective-permute-done.41.rest_16_), channel_id=1, source_target_pairs={{0,1},{1,0},{2,3},{3,2},{4,5},{5,4},{6,7},{7,6},{8,9},{9,8},{10,11... | collective-permute-start | bytes 393224 | tf_op jit(solution)/shard_map/ppermute | solution.py:296
  114.4 1.8 %collective-permute-start.46 = (f32[128,256]{1,0:T(8,128)S(1)}, f32[128,256]{1,0:T(8,128)S(1)}, u32[]{:S(2)}, u32[]{:S(2)}) collective-permute-start(f32[128,256]{1,0:T(8,128)S(1)} %collective-permute-done.45.rest_20_), channel_id=1, source_target_pairs={{0,1},{1,0},{2,3},{3,2},{4,5},{5,4},{6,7},{7,6},{8,9},{9,8},{10,11... | collective-permute-start | bytes 393224 | tf_op jit(solution)/shard_map/ppermute | solution.py:296
  117.2 1.8 %collective-permute-start.50 = (f32[128,256]{1,0:T(8,128)S(1)}, f32[128,256]{1,0:T(8,128)S(1)}, u32[]{:S(2)}, u32[]{:S(2)}) collective-permute-start(f32[128,256]{1,0:T(8,128)S(1)} %collective-permute-done.49.rest_24_), channel_id=1, source_target_pairs={{0,1},{1,0},{2,3},{3,2},{4,5},{5,4},{6,7},{7,6},{8,9},{9,8},{10,11... | collective-permute-start | bytes 393224 | tf_op jit(solution)/shard_map/ppermute | solution.py:296
  120.0 1.8 %collective-permute-start.54 = (f32[128,256]{1,0:T(8,128)S(1)}, f32[128,256]{1,0:T(8,128)S(1)}, u32[]{:S(2)}, u32[]{:S(2)}) collective-permute-start(f32[128,256]{1,0:T(8,128)S(1)} %collective-permute-done.53.rest_28_), channel_id=1, source_target_pairs={{0,1},{1,0},{2,3},{3,2},{4,5},{5,4},{6,7},{7,6},{8,9},{9,8},{10,11... | collective-permute-start | bytes 393224 | tf_op jit(solution)/shard_map/ppermute | solution.py:296
  122.8 1.8 %collective-permute-start.32 = (f32[128,256]{1,0:T(8,128)S(1)}, f32[128,256]{1,0:T(8,128)S(1)}, u32[]{:S(2)}, u32[]{:S(2)}) collective-permute-start(f32[128,256]{1,0:T(8,128)S(1)} %collective-permute-done.31.rest_6_), channel_id=1, source_target_pairs={{0,1},{1,0},{2,3},{3,2},{4,5},{5,4},{6,7},{7,6},{8,9},{9,8},{10,11... | collective-permute-start | bytes 393224 | tf_op jit(solution)/shard_map/ppermute | solution.py:296
  125.6 1.8 %collective-permute-start.40 = (f32[128,256]{1,0:T(8,128)S(1)}, f32[128,256]{1,0:T(8,128)S(1)}, u32[]{:S(2)}, u32[]{:S(2)}) collective-permute-start(f32[128,256]{1,0:T(8,128)S(1)} %collective-permute-done.39.rest_14_), channel_id=1, source_target_pairs={{0,1},{1,0},{2,3},{3,2},{4,5},{5,4},{6,7},{7,6},{8,9},{9,8},{10,11... | collective-permute-start | bytes 393224 | tf_op jit(solution)/shard_map/ppermute | solution.py:296
  128.4 1.8 %collective-permute-start.48 = (f32[128,256]{1,0:T(8,128)S(1)}, f32[128,256]{1,0:T(8,128)S(1)}, u32[]{:S(2)}, u32[]{:S(2)}) collective-permute-start(f32[128,256]{1,0:T(8,128)S(1)} %collective-permute-done.47.rest_22_), channel_id=1, source_target_pairs={{0,1},{1,0},{2,3},{3,2},{4,5},{5,4},{6,7},{7,6},{8,9},{9,8},{10,11... | collective-permute-start | bytes 393224 | tf_op jit(solution)/shard_map/ppermute | solution.py:296
  131.2 1.8 %collective-permute-start.56 = (f32[128,256]{1,0:T(8,128)S(1)}, f32[128,256]{1,0:T(8,128)S(1)}, u32[]{:S(2)}, u32[]{:S(2)}) collective-permute-start(f32[128,256]{1,0:T(8,128)S(1)} %collective-permute-done.55.rest_30_), channel_id=1, source_target_pairs={{0,1},{1,0},{2,3},{3,2},{4,5},{5,4},{6,7},{7,6},{8,9},{9,8},{10,11... | collective-permute-start | bytes 393224 | tf_op jit(solution)/shard_map/ppermute | solution.py:296
  134.1 1.4 collective-permute-done.48.rest_23_
  136.9 6.8 %conv_two.1 = f32[1024,256]{1,0:T(8,128)} custom-call(s32[8,16]{1,0:T(8,128)S(1)} %bitcast.9, bf16[8,256,2048]{2,1,0:T(8,128)(2,1)S(1)} %get-tuple-element.41.a_ref, f32[8,128,128]{2,1,0:T(8,128)S(1)} %get-tuple-element.42.s_ref, f32[128,256]{1,0:T(8,128)S(1)} %get-tuple-element.69.rest_0_, f32[128,256]{1,0:T(8,128)S(1)} %collective-permute-done.26.rest_1_, ...), custom_call_target="tpu_custom_call" | custom-call | flops 3221225472 | bytes 12582912 | tf_op jit(solution)/shard_map/conv_two/pallas_call | solution.py:281
  (90 shorter events, 19.3 us)
Async XLA Ops:
  3.7 10.2 %collective-permute-start = (f32[512,128]{1,0:T(8,128)S(1)}, f32[512,128]{1,0:T(8,128)S(1)}, u32[]{:S(2)}, u32[]{:S(2)}) collective-permute-start(f32[512,128]{1,0:T(8,128)S(1)} %get-tuple-element.43.rest_0_), channel_id=1, source_target_pairs={{0,1},{1,0},{2,3},{3,2},{4,5},{5,4},{6,7},{7,6},{8,9},{9,8},{10,11... | collective-permute-start | bytes 786440 | tf_op jit(solution)/shard_map/ppermute | solution.py:296
  6.7 9.2 %collective-permute-start.1 = (f32[512,128]{1,0:T(8,128)S(1)}, f32[512,128]{1,0:T(8,128)S(1)}, u32[]{:S(2)}, u32[]{:S(2)}) collective-permute-start(f32[512,128]{1,0:T(8,128)S(1)} %get-tuple-element.43.rest_0_), channel_id=1, source_target_pairs={{0,2},{1,3},{2,0},{3,1},{4,6},{5,7},{6,4},{7,5},{8,10},{9,11},{10,... | collective-permute-start | bytes 786440 | tf_op jit(solution)/shard_map/ppermute | solution.py:296
  8.2 13.3 %collective-permute-start.4 = (f32[512,128]{1,0:T(8,128)S(1)}, f32[512,128]{1,0:T(8,128)S(1)}, u32[]{:S(2)}, u32[]{:S(2)}) collective-permute-start(f32[512,128]{1,0:T(8,128)S(1)} %get-tuple-element.44.rest_4_), channel_id=1, source_target_pairs={{0,2},{1,3},{2,0},{3,1},{4,6},{5,7},{6,4},{7,5},{8,10},{9,11},{10,... | collective-permute-start | bytes 786440 | tf_op jit(solution)/shard_map/ppermute | solution.py:296
  8.7 12.8 %collective-permute-start.3 = (f32[512,128]{1,0:T(8,128)S(1)}, f32[512,128]{1,0:T(8,128)S(1)}, u32[]{:S(2)}, u32[]{:S(2)}) collective-permute-start(f32[512,128]{1,0:T(8,128)S(1)} %get-tuple-element.44.rest_4_), channel_id=1, source_target_pairs={{0,1},{1,0},{2,3},{3,2},{4,5},{5,4},{6,7},{7,6},{8,9},{9,8},{10,11... | collective-permute-start | bytes 786440 | tf_op jit(solution)/shard_map/ppermute | solution.py:296
  8.8 16.3 %collective-permute-start.13 = (f32[512,128]{1,0:T(8,128)S(1)}, f32[512,128]{1,0:T(8,128)S(1)}, u32[]{:S(2)}, u32[]{:S(2)}) collective-permute-start(f32[512,128]{1,0:T(8,128)S(1)} %get-tuple-element.53.rest_0_), channel_id=1, source_target_pairs={{0,1},{1,0},{2,3},{3,2},{4,5},{5,4},{6,7},{7,6},{8,9},{9,8},{10,11... | collective-permute-start | bytes 786440 | tf_op jit(solution)/shard_map/ppermute | solution.py:296
  13.9 13.3 %collective-permute-start.17 = (f32[512,128]{1,0:T(8,128)S(1)}, f32[512,128]{1,0:T(8,128)S(1)}, u32[]{:S(2)}, u32[]{:S(2)}) collective-permute-start(f32[512,128]{1,0:T(8,128)S(1)} %get-tuple-element.54.rest_4_), channel_id=1, source_target_pairs={{0,2},{1,3},{2,0},{3,1},{4,6},{5,7},{6,4},{7,5},{8,10},{9,11},{10,... | collective-permute-start | bytes 786440 | tf_op jit(solution)/shard_map/ppermute | solution.py:296
  15.9 16.8 %collective-permute-start.2 = (f32[512,128]{1,0:T(8,128)S(1)}, f32[512,128]{1,0:T(8,128)S(1)}, u32[]{:S(2)}, u32[]{:S(2)}) collective-permute-start(f32[512,128]{1,0:T(8,128)S(1)} %collective-permute-done.rest_1_), channel_id=1, source_target_pairs={{0,2},{1,3},{2,0},{3,1},{4,6},{5,7},{6,4},{7,5},{8,10},{9,11},{10,... | collective-permute-start | bytes 786440 | tf_op jit(solution)/shard_map/ppermute | solution.py:296
  21.5 17.6 %collective-permute-start.5 = (f32[512,128]{1,0:T(8,128)S(1)}, f32[512,128]{1,0:T(8,128)S(1)}, u32[]{:S(2)}, u32[]{:S(2)}) collective-permute-start(f32[512,128]{1,0:T(8,128)S(1)} %collective-permute-done.4.rest_6_), channel_id=1, source_target_pairs={{0,1},{1,0},{2,3},{3,2},{4,5},{5,4},{6,7},{7,6},{8,9},{9,8},{10,11... | collective-permute-start | bytes 786440 | tf_op jit(solution)/shard_map/ppermute | solution.py:296
  21.6 22.2 %collective-permute-start.14 = (f32[512,128]{1,0:T(8,128)S(1)}, f32[512,128]{1,0:T(8,128)S(1)}, u32[]{:S(2)}, u32[]{:S(2)}) collective-permute-start(f32[512,128]{1,0:T(8,128)S(1)} %get-tuple-element.53.rest_0_), channel_id=1, source_target_pairs={{0,2},{1,3},{2,0},{3,1},{4,6},{5,7},{6,4},{7,5},{8,10},{9,11},{10,... | collective-permute-start | bytes 786440 | tf_op jit(solution)/shard_map/ppermute | solution.py:296
  25.1 20.8 %collective-permute-start.16 = (f32[512,128]{1,0:T(8,128)S(1)}, f32[512,128]{1,0:T(8,128)S(1)}, u32[]{:S(2)}, u32[]{:S(2)}) collective-permute-start(f32[512,128]{1,0:T(8,128)S(1)} %get-tuple-element.54.rest_4_), channel_id=1, source_target_pairs={{0,1},{1,0},{2,3},{3,2},{4,5},{5,4},{6,7},{7,6},{8,9},{9,8},{10,11... | collective-permute-start | bytes 786440 | tf_op jit(solution)/shard_map/ppermute | solution.py:296
  27.1 18.9 %collective-permute-start.15 = (f32[512,128]{1,0:T(8,128)S(1)}, f32[512,128]{1,0:T(8,128)S(1)}, u32[]{:S(2)}, u32[]{:S(2)}) collective-permute-start(f32[512,128]{1,0:T(8,128)S(1)} %collective-permute-done.13.rest_1_), channel_id=1, source_target_pairs={{0,2},{1,3},{2,0},{3,1},{4,6},{5,7},{6,4},{7,5},{8,10},{9,11},{10,... | collective-permute-start | bytes 786440 | tf_op jit(solution)/shard_map/ppermute | solution.py:296
  32.7 16.0 %collective-permute-start.18 = (f32[512,128]{1,0:T(8,128)S(1)}, f32[512,128]{1,0:T(8,128)S(1)}, u32[]{:S(2)}, u32[]{:S(2)}) collective-permute-start(f32[512,128]{1,0:T(8,128)S(1)} %collective-permute-done.17.rest_6_), channel_id=1, source_target_pairs={{0,1},{1,0},{2,3},{3,2},{4,5},{5,4},{6,7},{7,6},{8,9},{9,8},{10,11... | collective-permute-start | bytes 786440 | tf_op jit(solution)/shard_map/ppermute | solution.py:296
  43.7 10.2 %collective-permute-start.6 = (f32[128,128]{1,0:T(8,128)S(1)}, f32[128,128]{1,0:T(8,128)S(1)}, u32[]{:S(2)}, u32[]{:S(2)}) collective-permute-start(f32[128,128]{1,0:T(8,128)S(1)} %get-tuple-element.46), channel_id=1, source_target_pairs={{0,4},{4,0},{8,12},{12,8},{16,20},{20,16},{24,28},{28,24},{1,5},{5... | collective-permute-start | bytes 196616 | tf_op jit(solution)/shard_map/ppermute | solution.py:296
  43.8 13.8 %collective-permute-start.7 = (f32[128,128]{1,0:T(8,128)S(1)}, f32[128,128]{1,0:T(8,128)S(1)}, u32[]{:S(2)}, u32[]{:S(2)}) collective-permute-start(f32[128,128]{1,0:T(8,128)S(1)} %get-tuple-element.47), channel_id=1, source_target_pairs={{0,8},{4,12},{8,0},{12,4},{16,24},{20,28},{24,16},{28,20},{1,9},{5... | collective-permute-start | bytes 196616 | tf_op jit(solution)/shard_map/ppermute | solution.py:296
  45.9 11.8 %collective-permute-start.8 = (f32[128,128]{1,0:T(8,128)S(1)}, f32[128,128]{1,0:T(8,128)S(1)}, u32[]{:S(2)}, u32[]{:S(2)}) collective-permute-start(f32[128,128]{1,0:T(8,128)S(1)} %get-tuple-element.48), channel_id=1, source_target_pairs={{0,12},{4,8},{8,4},{12,0},{16,28},{20,24},{24,20},{28,16},{1,13},{... | collective-permute-start | bytes 196616 | tf_op jit(solution)/shard_map/ppermute | solution.py:296
  46.0 12.0 %collective-permute-start.9 = (f32[128,128]{1,0:T(8,128)S(1)}, f32[128,128]{1,0:T(8,128)S(1)}, u32[]{:S(2)}, u32[]{:S(2)}) collective-permute-start(f32[128,128]{1,0:T(8,128)S(1)} %get-tuple-element.49), channel_id=1, source_target_pairs={{0,16},{4,20},{8,24},{12,28},{16,0},{20,4},{24,8},{28,12},{1,17},{... | collective-permute-start | bytes 196616 | tf_op jit(solution)/shard_map/ppermute | solution.py:296
  48.7 9.3 %collective-permute-start.10 = (f32[128,128]{1,0:T(8,128)S(1)}, f32[128,128]{1,0:T(8,128)S(1)}, u32[]{:S(2)}, u32[]{:S(2)}) collective-permute-start(f32[128,128]{1,0:T(8,128)S(1)} %get-tuple-element.50), channel_id=1, source_target_pairs={{0,20},{4,16},{8,28},{12,24},{16,4},{20,0},{24,12},{28,8},{1,21},{... | collective-permute-start | bytes 196616 | tf_op jit(solution)/shard_map/ppermute | solution.py:296
  57.7 7.2 %collective-permute-start.19 = (f32[128,128]{1,0:T(8,128)S(1)}, f32[128,128]{1,0:T(8,128)S(1)}, u32[]{:S(2)}, u32[]{:S(2)}) collective-permute-start(f32[128,128]{1,0:T(8,128)S(1)} %get-tuple-element.58), channel_id=1, source_target_pairs={{0,4},{4,0},{8,12},{12,8},{16,20},{20,16},{24,28},{28,24},{1,5},{5... | collective-permute-start | bytes 196616 | tf_op jit(solution)/shard_map/ppermute | solution.py:296
  58.0 8.0 %collective-permute-start.20 = (f32[128,128]{1,0:T(8,128)S(1)}, f32[128,128]{1,0:T(8,128)S(1)}, u32[]{:S(2)}, u32[]{:S(2)}) collective-permute-start(f32[128,128]{1,0:T(8,128)S(1)} %get-tuple-element.59), channel_id=1, source_target_pairs={{0,8},{4,12},{8,0},{12,4},{16,24},{20,28},{24,16},{28,20},{1,9},{5... | collective-permute-start | bytes 196616 | tf_op jit(solution)/shard_map/ppermute | solution.py:296
  58.0 10.1 %collective-permute-start.21 = (f32[128,128]{1,0:T(8,128)S(1)}, f32[128,128]{1,0:T(8,128)S(1)}, u32[]{:S(2)}, u32[]{:S(2)}) collective-permute-start(f32[128,128]{1,0:T(8,128)S(1)} %get-tuple-element.60), channel_id=1, source_target_pairs={{0,12},{4,8},{8,4},{12,0},{16,28},{20,24},{24,20},{28,16},{1,13},{... | collective-permute-start | bytes 196616 | tf_op jit(solution)/shard_map/ppermute | solution.py:296
  60.4 7.7 %collective-permute-start.22 = (f32[128,128]{1,0:T(8,128)S(1)}, f32[128,128]{1,0:T(8,128)S(1)}, u32[]{:S(2)}, u32[]{:S(2)}) collective-permute-start(f32[128,128]{1,0:T(8,128)S(1)} %get-tuple-element.61), channel_id=1, source_target_pairs={{0,16},{4,20},{8,24},{12,28},{16,0},{20,4},{24,8},{28,12},{1,17},{... | collective-permute-start | bytes 196616 | tf_op jit(solution)/shard_map/ppermute | solution.py:296
  63.6 10.0 %collective-permute-start.23 = (f32[128,128]{1,0:T(8,128)S(1)}, f32[128,128]{1,0:T(8,128)S(1)}, u32[]{:S(2)}, u32[]{:S(2)}) collective-permute-start(f32[128,128]{1,0:T(8,128)S(1)} %get-tuple-element.62), channel_id=1, source_target_pairs={{0,20},{4,16},{8,28},{12,24},{16,4},{20,0},{24,12},{28,8},{1,21},{... | collective-permute-start | bytes 196616 | tf_op jit(solution)/shard_map/ppermute | solution.py:296
  64.9 8.6 %collective-permute-start.24 = (f32[128,128]{1,0:T(8,128)S(1)}, f32[128,128]{1,0:T(8,128)S(1)}, u32[]{:S(2)}, u32[]{:S(2)}) collective-permute-start(f32[128,128]{1,0:T(8,128)S(1)} %get-tuple-element.63), channel_id=1, source_target_pairs={{0,24},{4,28},{8,16},{12,20},{16,8},{20,12},{24,0},{28,4},{1,25},{... | collective-permute-start | bytes 196616 | tf_op jit(solution)/shard_map/ppermute | solution.py:296
  66.0 7.6 %collective-permute-start.25 = (f32[128,128]{1,0:T(8,128)S(1)}, f32[128,128]{1,0:T(8,128)S(1)}, u32[]{:S(2)}, u32[]{:S(2)}) collective-permute-start(f32[128,128]{1,0:T(8,128)S(1)} %get-tuple-element.64), channel_id=1, source_target_pairs={{0,28},{4,24},{8,20},{12,16},{16,12},{20,8},{24,4},{28,0},{1,29},{... | collective-permute-start | bytes 196616 | tf_op jit(solution)/shard_map/ppermute | solution.py:296
  79.7 7.9 %collective-permute-start.27 = (f32[128,256]{1,0:T(8,128)S(1)}, f32[128,256]{1,0:T(8,128)S(1)}, u32[]{:S(2)}, u32[]{:S(2)}) collective-permute-start(f32[128,256]{1,0:T(8,128)S(1)} %get-tuple-element.69.rest_0_), channel_id=1, source_target_pairs={{0,2},{1,3},{2,0},{3,1},{4,6},{5,7},{6,4},{7,5},{8,10},{9,11},{10,... | collective-permute-start | bytes 393224 | tf_op jit(solution)/shard_map/ppermute | solution.py:296
  81.2 12.2 %collective-permute-start.33 = (f32[128,256]{1,0:T(8,128)S(1)}, f32[128,256]{1,0:T(8,128)S(1)}, u32[]{:S(2)}, u32[]{:S(2)}) collective-permute-start(f32[128,256]{1,0:T(8,128)S(1)} %get-tuple-element.71), channel_id=1, source_target_pairs={{0,8},{4,12},{8,0},{12,4},{16,24},{20,28},{24,16},{28,20},{1,9},{5... | collective-permute-start | bytes 393224 | tf_op jit(solution)/shard_map/ppermute | solution.py:296
  84.6 11.3 %collective-permute-start.37 = (f32[128,256]{1,0:T(8,128)S(1)}, f32[128,256]{1,0:T(8,128)S(1)}, u32[]{:S(2)}, u32[]{:S(2)}) collective-permute-start(f32[128,256]{1,0:T(8,128)S(1)} %get-tuple-element.72), channel_id=1, source_target_pairs={{0,12},{4,8},{8,4},{12,0},{16,28},{20,24},{24,20},{28,16},{1,13},{... | collective-permute-start | bytes 393224 | tf_op jit(solution)/shard_map/ppermute | solution.py:296
  84.7 11.2 %collective-permute-start.41 = (f32[128,256]{1,0:T(8,128)S(1)}, f32[128,256]{1,0:T(8,128)S(1)}, u32[]{:S(2)}, u32[]{:S(2)}) collective-permute-start(f32[128,256]{1,0:T(8,128)S(1)} %get-tuple-element.73), channel_id=1, source_target_pairs={{0,16},{4,20},{8,24},{12,28},{16,0},{20,4},{24,8},{28,12},{1,17},{... | collective-permute-start | bytes 393224 | tf_op jit(solution)/shard_map/ppermute | solution.py:296
  87.6 17.9 %collective-permute-start.45 = (f32[128,256]{1,0:T(8,128)S(1)}, f32[128,256]{1,0:T(8,128)S(1)}, u32[]{:S(2)}, u32[]{:S(2)}) collective-permute-start(f32[128,256]{1,0:T(8,128)S(1)} %get-tuple-element.74), channel_id=1, source_target_pairs={{0,20},{4,16},{8,28},{12,24},{16,4},{20,0},{24,12},{28,8},{1,21},{... | collective-permute-start | bytes 393224 | tf_op jit(solution)/shard_map/ppermute | solution.py:296
  87.8 19.2 %collective-permute-start.49 = (f32[128,256]{1,0:T(8,128)S(1)}, f32[128,256]{1,0:T(8,128)S(1)}, u32[]{:S(2)}, u32[]{:S(2)}) collective-permute-start(f32[128,256]{1,0:T(8,128)S(1)} %get-tuple-element.75), channel_id=1, source_target_pairs={{0,24},{4,28},{8,16},{12,20},{16,8},{20,12},{24,0},{28,4},{1,25},{... | collective-permute-start | bytes 393224 | tf_op jit(solution)/shard_map/ppermute | solution.py:296
  93.5 14.5 %collective-permute-start.53 = (f32[128,256]{1,0:T(8,128)S(1)}, f32[128,256]{1,0:T(8,128)S(1)}, u32[]{:S(2)}, u32[]{:S(2)}) collective-permute-start(f32[128,256]{1,0:T(8,128)S(1)} %get-tuple-element.76), channel_id=1, source_target_pairs={{0,28},{4,24},{8,20},{12,16},{16,12},{20,8},{24,4},{28,0},{1,29},{... | collective-permute-start | bytes 393224 | tf_op jit(solution)/shard_map/ppermute | solution.py:296
  95.9 13.1 %collective-permute-start.28 = (f32[128,256]{1,0:T(8,128)S(1)}, f32[128,256]{1,0:T(8,128)S(1)}, u32[]{:S(2)}, u32[]{:S(2)}) collective-permute-start(f32[128,256]{1,0:T(8,128)S(1)} %collective-permute-done.26.rest_1_), channel_id=1, source_target_pairs={{0,2},{1,3},{2,0},{3,1},{4,6},{5,7},{6,4},{7,5},{8,10},{9,11},{10,... | collective-permute-start | bytes 393224 | tf_op jit(solution)/shard_map/ppermute | solution.py:296
  95.9 13.6 %collective-permute-start.30 = (f32[128,256]{1,0:T(8,128)S(1)}, f32[128,256]{1,0:T(8,128)S(1)}, u32[]{:S(2)}, u32[]{:S(2)}) collective-permute-start(f32[128,256]{1,0:T(8,128)S(1)} %collective-permute-done.29.rest_4_), channel_id=1, source_target_pairs={{0,1},{1,0},{2,3},{3,2},{4,5},{5,4},{6,7},{7,6},{8,9},{9,8},{10,11... | collective-permute-start | bytes 393224 | tf_op jit(solution)/shard_map/ppermute | solution.py:296
  109.0 7.1 %collective-permute-start.38 = (f32[128,256]{1,0:T(8,128)S(1)}, f32[128,256]{1,0:T(8,128)S(1)}, u32[]{:S(2)}, u32[]{:S(2)}) collective-permute-start(f32[128,256]{1,0:T(8,128)S(1)} %collective-permute-done.37.rest_12_), channel_id=1, source_target_pairs={{0,1},{1,0},{2,3},{3,2},{4,5},{5,4},{6,7},{7,6},{8,9},{9,8},{10,11... | collective-permute-start | bytes 393224 | tf_op jit(solution)/shard_map/ppermute | solution.py:296
  109.6 7.6 %collective-permute-start.39 = (f32[128,256]{1,0:T(8,128)S(1)}, f32[128,256]{1,0:T(8,128)S(1)}, u32[]{:S(2)}, u32[]{:S(2)}) collective-permute-start(f32[128,256]{1,0:T(8,128)S(1)} %collective-permute-done.37.rest_12_), channel_id=1, source_target_pairs={{0,2},{1,3},{2,0},{3,1},{4,6},{5,7},{6,4},{7,5},{8,10},{9,11},{10,... | collective-permute-start | bytes 393224 | tf_op jit(solution)/shard_map/ppermute | solution.py:296
  111.0 7.9 %collective-permute-start.42 = (f32[128,256]{1,0:T(8,128)S(1)}, f32[128,256]{1,0:T(8,128)S(1)}, u32[]{:S(2)}, u32[]{:S(2)}) collective-permute-start(f32[128,256]{1,0:T(8,128)S(1)} %collective-permute-done.41.rest_16_), channel_id=1, source_target_pairs={{0,1},{1,0},{2,3},{3,2},{4,5},{5,4},{6,7},{7,6},{8,9},{9,8},{10,11... | collective-permute-start | bytes 393224 | tf_op jit(solution)/shard_map/ppermute | solution.py:296
  113.3 6.7 %collective-permute-start.43 = (f32[128,256]{1,0:T(8,128)S(1)}, f32[128,256]{1,0:T(8,128)S(1)}, u32[]{:S(2)}, u32[]{:S(2)}) collective-permute-start(f32[128,256]{1,0:T(8,128)S(1)} %collective-permute-done.41.rest_16_), channel_id=1, source_target_pairs={{0,2},{1,3},{2,0},{3,1},{4,6},{5,7},{6,4},{7,5},{8,10},{9,11},{10,... | collective-permute-start | bytes 393224 | tf_op jit(solution)/shard_map/ppermute | solution.py:296
  114.4 7.4 %collective-permute-start.46 = (f32[128,256]{1,0:T(8,128)S(1)}, f32[128,256]{1,0:T(8,128)S(1)}, u32[]{:S(2)}, u32[]{:S(2)}) collective-permute-start(f32[128,256]{1,0:T(8,128)S(1)} %collective-permute-done.45.rest_20_), channel_id=1, source_target_pairs={{0,1},{1,0},{2,3},{3,2},{4,5},{5,4},{6,7},{7,6},{8,9},{9,8},{10,11... | collective-permute-start | bytes 393224 | tf_op jit(solution)/shard_map/ppermute | solution.py:296
  116.2 6.7 %collective-permute-start.47 = (f32[128,256]{1,0:T(8,128)S(1)}, f32[128,256]{1,0:T(8,128)S(1)}, u32[]{:S(2)}, u32[]{:S(2)}) collective-permute-start(f32[128,256]{1,0:T(8,128)S(1)} %collective-permute-done.45.rest_20_), channel_id=1, source_target_pairs={{0,2},{1,3},{2,0},{3,1},{4,6},{5,7},{6,4},{7,5},{8,10},{9,11},{10,... | collective-permute-start | bytes 393224 | tf_op jit(solution)/shard_map/ppermute | solution.py:296
  117.2 7.4 %collective-permute-start.50 = (f32[128,256]{1,0:T(8,128)S(1)}, f32[128,256]{1,0:T(8,128)S(1)}, u32[]{:S(2)}, u32[]{:S(2)}) collective-permute-start(f32[128,256]{1,0:T(8,128)S(1)} %collective-permute-done.49.rest_24_), channel_id=1, source_target_pairs={{0,1},{1,0},{2,3},{3,2},{4,5},{5,4},{6,7},{7,6},{8,9},{9,8},{10,11... | collective-permute-start | bytes 393224 | tf_op jit(solution)/shard_map/ppermute | solution.py:296
  119.0 6.7 %collective-permute-start.51 = (f32[128,256]{1,0:T(8,128)S(1)}, f32[128,256]{1,0:T(8,128)S(1)}, u32[]{:S(2)}, u32[]{:S(2)}) collective-permute-start(f32[128,256]{1,0:T(8,128)S(1)} %collective-permute-done.49.rest_24_), channel_id=1, source_target_pairs={{0,2},{1,3},{2,0},{3,1},{4,6},{5,7},{6,4},{7,5},{8,10},{9,11},{10,... | collective-permute-start | bytes 393224 | tf_op jit(solution)/shard_map/ppermute | solution.py:296
  120.0 7.4 %collective-permute-start.54 = (f32[128,256]{1,0:T(8,128)S(1)}, f32[128,256]{1,0:T(8,128)S(1)}, u32[]{:S(2)}, u32[]{:S(2)}) collective-permute-start(f32[128,256]{1,0:T(8,128)S(1)} %collective-permute-done.53.rest_28_), channel_id=1, source_target_pairs={{0,1},{1,0},{2,3},{3,2},{4,5},{5,4},{6,7},{7,6},{8,9},{9,8},{10,11... | collective-permute-start | bytes 393224 | tf_op jit(solution)/shard_map/ppermute | solution.py:296
  121.8 6.7 %collective-permute-start.55 = (f32[128,256]{1,0:T(8,128)S(1)}, f32[128,256]{1,0:T(8,128)S(1)}, u32[]{:S(2)}, u32[]{:S(2)}) collective-permute-start(f32[128,256]{1,0:T(8,128)S(1)} %collective-permute-done.53.rest_28_), channel_id=1, source_target_pairs={{0,2},{1,3},{2,0},{3,1},{4,6},{5,7},{6,4},{7,5},{8,10},{9,11},{10,... | collective-permute-start | bytes 393224 | tf_op jit(solution)/shard_map/ppermute | solution.py:296
  122.8 7.4 %collective-permute-start.32 = (f32[128,256]{1,0:T(8,128)S(1)}, f32[128,256]{1,0:T(8,128)S(1)}, u32[]{:S(2)}, u32[]{:S(2)}) collective-permute-start(f32[128,256]{1,0:T(8,128)S(1)} %collective-permute-done.31.rest_6_), channel_id=1, source_target_pairs={{0,1},{1,0},{2,3},{3,2},{4,5},{5,4},{6,7},{7,6},{8,9},{9,8},{10,11... | collective-permute-start | bytes 393224 | tf_op jit(solution)/shard_map/ppermute | solution.py:296
  124.6 6.7 %collective-permute-start.36 = (f32[128,256]{1,0:T(8,128)S(1)}, f32[128,256]{1,0:T(8,128)S(1)}, u32[]{:S(2)}, u32[]{:S(2)}) collective-permute-start(f32[128,256]{1,0:T(8,128)S(1)} %collective-permute-done.34.rest_9_), channel_id=1, source_target_pairs={{0,2},{1,3},{2,0},{3,1},{4,6},{5,7},{6,4},{7,5},{8,10},{9,11},{10,... | collective-permute-start | bytes 393224 | tf_op jit(solution)/shard_map/ppermute | solution.py:296
  125.6 7.4 %collective-permute-start.40 = (f32[128,256]{1,0:T(8,128)S(1)}, f32[128,256]{1,0:T(8,128)S(1)}, u32[]{:S(2)}, u32[]{:S(2)}) collective-permute-start(f32[128,256]{1,0:T(8,128)S(1)} %collective-permute-done.39.rest_14_), channel_id=1, source_target_pairs={{0,1},{1,0},{2,3},{3,2},{4,5},{5,4},{6,7},{7,6},{8,9},{9,8},{10,11... | collective-permute-start | bytes 393224 | tf_op jit(solution)/shard_map/ppermute | solution.py:296
  127.4 6.7 %collective-permute-start.44 = (f32[128,256]{1,0:T(8,128)S(1)}, f32[128,256]{1,0:T(8,128)S(1)}, u32[]{:S(2)}, u32[]{:S(2)}) collective-permute-start(f32[128,256]{1,0:T(8,128)S(1)} %collective-permute-done.42.rest_17_), channel_id=1, source_target_pairs={{0,2},{1,3},{2,0},{3,1},{4,6},{5,7},{6,4},{7,5},{8,10},{9,11},{10,... | collective-permute-start | bytes 393224 | tf_op jit(solution)/shard_map/ppermute | solution.py:296
  128.4 7.0 %collective-permute-start.48 = (f32[128,256]{1,0:T(8,128)S(1)}, f32[128,256]{1,0:T(8,128)S(1)}, u32[]{:S(2)}, u32[]{:S(2)}) collective-permute-start(f32[128,256]{1,0:T(8,128)S(1)} %collective-permute-done.47.rest_22_), channel_id=1, source_target_pairs={{0,1},{1,0},{2,3},{3,2},{4,5},{5,4},{6,7},{7,6},{8,9},{9,8},{10,11... | collective-permute-start | bytes 393224 | tf_op jit(solution)/shard_map/ppermute | solution.py:296
  (17 other events, 170.8 us)
